TPU v7x, 1024 devices: a whole 4x4x32 slice. The times are simulated.
1024 devices in a mesh: dp: 64 (over z, y_lo), mp: 16 (over x, y_hi, core).
Axes of the slice: x: 4, y: 4 (y_hi: 2, y_lo: 2; y = y_hi * 2 + y_lo), z: 32, core: 2. Of those that a mesh axis runs over, the one named last changes fastest.
Arguments:
- layer_input: bfloat16 [64, 16, 8, 32, 256], P('dp', 'mp'), may hold values from -6 to 6
- hidden_pre: bfloat16 [64, 16, 8, 32, 256], P('dp', 'mp'), may hold values from -6 to 6
- out_grad: bfloat16 [64, 16, 8, 32, 256], P('dp', 'mp'), may hold values from -0.03125 to 0.03125
- weight_second: bfloat16 [256, 6912], replicated, may hold values from -0.078125 to 0.078125
Outputs:
- grad_second: float32 [256, 6912], P('mp')
- grad_first: float32 [256, 6912], P('mp')
All inputs are finite; a program needn't handle non-finite values.
Results may differ from a plain program's by a relative error of at most 0.0029.
Values may be sent and summed in bfloat16 or wider, within the bound.
No kernel may reach another device: no remote copies, remote signals or barrier semaphores. Data moves between devices by JAX's collectives and lax.ppermute only.
A program may use at most 32 MiB of HBM per device.

v0:
```python
import jax
import jax.numpy as jnp
from jax import lax
from jax.sharding import PartitionSpec as P


def extended(block, sides, width):
    for axis, dim in sides:
        count = lax.axis_size(axis)
        forward = [(i, i + 1) for i in range(count - 1)]
        backward = [(target, source) for source, target in forward]
        low = lax.ppermute(
            lax.slice_in_dim(block, block.shape[dim] - width, None, axis=dim), axis, forward
        )
        high = lax.ppermute(lax.slice_in_dim(block, 0, width, axis=dim), axis, backward)
        block = jnp.concatenate([low, block, high], axis=dim)
    return block


def fold_taps(piece, start, grad_pad):
    planes, height, width, chans = piece.shape
    owned = grad_pad.shape[3]
    flat = piece.reshape(planes * height * width, chans)
    columns = []
    for shift_x in range(3):
        block = lax.dynamic_slice_in_dim(grad_pad, start + 2 - shift_x, planes, 0)
        for shift_y in range(3):
            for shift_z in range(3):
                tap_grad = block[
                    :, 2 - shift_y : 2 - shift_y + height, 2 - shift_z : 2 - shift_z + width, :
                ]
                tap_grad = tap_grad.reshape(planes * height * width, owned)
                columns.append(
                    lax.dot_general(
                        tap_grad, flat, (((0,), (0,)), ((), ())), preferred_element_type=jnp.float32
                    )
                )
    term = jnp.stack(columns, 1)
    return term.reshape(owned, 27 * chans)


def pad_volume(volume):
    return jnp.pad(volume, ((1, 1), (1, 1), (1, 1), (0, 0)))


def regroup(grad):
    return lax.all_to_all(grad, "mp", split_axis=3, concat_axis=0, tiled=True)


def local(layer_input, hidden_pre, out_grad, weight_second):
    first_in = layer_input[0]
    pre_local = hidden_pre[0]
    grad_local = out_grad[0]
    planes, height, width, chans = grad_local.shape
    kernel = weight_second.reshape(weight_second.shape[0], 27, chans)
    grad_filter = regroup(grad_local)
    grad_pad = pad_volume(grad_filter)
    second_input = jnp.maximum(pre_local, 0)
    grad_two = fold_taps(
        lax.all_gather(second_input, "mp", axis=0, tiled=True), jnp.int32(0), grad_pad
    )
    rim = extended(grad_local, (("mp", 0),), 1)
    padded = jnp.pad(rim, ((0, 0), (1, 1), (1, 1), (0, 0)))
    input_grad = jnp.zeros((planes * height * width, chans), jnp.float32)
    tap_index = 0
    for shift_x in range(3):
        for shift_y in range(3):
            for shift_z in range(3):
                tap_grad = padded[
                    2 - shift_x : 2 - shift_x + planes,
                    2 - shift_y : 2 - shift_y + height,
                    2 - shift_z : 2 - shift_z + width,
                    :,
                ]
                tap_grad = tap_grad.reshape(planes * height * width, chans)
                input_grad = input_grad + jnp.dot(
                    tap_grad, kernel[:, tap_index, :], preferred_element_type=jnp.float32
                )
                tap_index = tap_index + 1
    input_grad = input_grad.reshape(planes, height, width, chans)
    hidden_grad = jnp.where(pre_local > 0, input_grad, 0.0).astype(jnp.bfloat16)
    hidden_filter = regroup(hidden_grad)
    hidden_pad = pad_volume(hidden_filter)
    grad_one = fold_taps(
        lax.all_gather(first_in, "mp", axis=0, tiled=True), jnp.int32(0), hidden_pad
    )
    grad_two, grad_one = lax.psum((grad_two, grad_one), "dp")
    return (grad_two, grad_one)


def solution(mesh):
    return jax.shard_map(
        local,
        mesh=mesh,
        in_specs=(
            P("dp", "mp", None, None, None),
            P("dp", "mp", None, None, None),
            P("dp", "mp", None, None, None),
            P(),
        ),
        out_specs=(P("mp", None), P("mp", None)),
        check_vma=False,
    )
```

profile of v0, /device:TPU:6, one launch (start us, length us, event | category | flops | bytes accessed | tf_op | source)
XLA Modules:
  0.0 746.1 jit_solution(6252934760717620533)
XLA Ops:
  7.2 1.9 collective-permute-start
  9.1 6.0 collective-permute-start.1
  15.2 1.2 copy.110
  16.5 1.2 reshape.285
  17.7 12.3 %all-to-all-start = ((bf16[16,2,2048]{2,1,0:T(2,128)(2,1)}), bf16[16,2,2048]{2,1,0:T(2,128)(2,1)}, u32[]{:S(2)}, u32[]{:S(2)}) async-start(bf16[16,2,2048]{2,1,0:T(2,128)(2,1)} %reshape.285), calls=%async_computation | async-start | bytes 262144 | tf_op jit(solution)/shard_map/all_to_all | solution.py:47
  30.0 5.0 copy.114
  35.0 1.2 select_maximum_fusion
  37.8 1.1 fusion.112
  42.8 1.1 fusion.111
  45.1 1.2 reshape.287
  46.2 7.2 all-to-all-start.1
  53.5 1.6 broadcast_maximum_fusion
  55.3 1.2 reshape.286
  56.7 3.2 all-to-all-done.1
  60.3 46.0 %all-gather.7.cloned.1.call-done = bf16[16,1,8,32,256]{4,3,2,1,0:T(8,128)(2,1)} async-done(((bf16[1,1,8,32,256]{4,3,2,1,0:T(8,128)(2,1)}), bf16[16,1,8,32,256]{4,3,2,1,0:T(8,128)(2,1)}) %all-gather.7.cloned.1.call-update) | async-done | bytes 2097168 | tf_op jit(solution)/shard_map/all_gather | solution.py:85
  106.3 2.6 fusion.278
  129.0 1.1 fusion.422
  130.9 0.9 fusion.434
  132.6 62.1 %all-gather.5.cloned.1.call-done = bf16[16,1,8,32,256]{4,3,2,1,0:T(8,128)(2,1)} async-done(((bf16[1,1,8,32,256]{4,3,2,1,0:T(8,128)(2,1)}), bf16[16,1,8,32,256]{4,3,2,1,0:T(8,128)(2,1)}) %all-gather.5.cloned.1.call-update) | async-done | bytes 2097168 | tf_op jit(solution)/shard_map/all_gather | solution.py:60
  194.7 2.6 fusion.116
  217.4 0.9 fusion.260
  220.9 515.1 %all-reduce.6.cloned.1.call-done = (f32[16,6912]{1,0:T(8,128)}, f32[16,6912]{1,0:T(8,128)}) async-done(((f32[16,6912]{1,0:T(8,128)}, f32[16,6912]{1,0:T(8,128)}), (f32[16,6912]{1,0:T(8,128)}, f32[16,6912]{1,0:T(8,128)})) %all-reduce.6.cloned.1.call-update) | async-done | bytes 884752 | tf_op jit(solution)/shard_map/psum | solution.py:87
  736.0 1.8 copy.266
  737.8 1.8 copy.267
  (100 shorter events, 51.3 us)
Async XLA Ops:
  7.2 99.1 %all-gather.7.cloned.1.call-start = ((), (), s32[]{:S(2)}) async-start(), calls=%async_computation.3 | async-start | bytes 2228224 | tf_op jit(solution)/shard_map/all_gather | solution.py:85
  7.2 27.7 %collective-permute-start = (bf16[1,8,32,256]{3,2,1,0:T(8,128)(2,1)}, bf16[1,8,32,256]{3,2,1,0:T(8,128)(2,1)}, u32[]{:S(2)}, u32[]{:S(2)}) collective-permute-start(bf16[1,8,32,256]{3,2,1,0:T(8,128)(2,1)} %bitcast.1036), channel_id=1, source_target_pairs={{0,1},{1,2},{2,3},{3,4},{4,5},{5,6},{6,7},{7,8},{8,9},{9,10},{10,1... | collective-permute-start | bytes 393224 | tf_op jit(solution)/shard_map/ppermute | solution.py:12
  9.1 25.8 %collective-permute-start.1 = (bf16[1,8,32,256]{3,2,1,0:T(8,128)(2,1)}, bf16[1,8,32,256]{3,2,1,0:T(8,128)(2,1)}, u32[]{:S(2)}, u32[]{:S(2)}) collective-permute-start(bf16[1,8,32,256]{3,2,1,0:T(8,128)(2,1)} %bitcast.1037), channel_id=1, source_target_pairs={{1,0},{2,1},{3,2},{4,3},{5,4},{6,5},{7,6},{8,7},{9,8},{10,9},{11,1... | collective-permute-start | bytes 393224 | tf_op jit(solution)/shard_map/ppermute | solution.py:15
  17.7 28.6 %all-to-all-start = ((bf16[16,2,2048]{2,1,0:T(2,128)(2,1)}), bf16[16,2,2048]{2,1,0:T(2,128)(2,1)}, u32[]{:S(2)}, u32[]{:S(2)}) async-start(bf16[16,2,2048]{2,1,0:T(2,128)(2,1)} %reshape.285), calls=%async_computation | async-start | bytes 262144 | tf_op jit(solution)/shard_map/all_to_all | solution.py:47
  39.4 1.4 copy-start.2
  42.6 2.1 copy-start.3
  46.2 13.7 %all-to-all-start.1 = ((bf16[16,2,2048]{2,1,0:T(2,128)(2,1)}), bf16[16,2,2048]{2,1,0:T(2,128)(2,1)S(1)}, u32[]{:S(2)}, u32[]{:S(2)}) async-start(bf16[16,2,2048]{2,1,0:T(2,128)(2,1)} %reshape.287), calls=%async_computation.1 | async-start | bytes 262144 | tf_op jit(solution)/shard_map/all_to_all | solution.py:47
  53.5 141.3 %all-gather.5.cloned.1.call-start = ((), (), s32[]{:S(2)}) async-start(), calls=%async_computation.2 | async-start | bytes 2228224 | tf_op jit(solution)/shard_map/all_gather | solution.py:60
  55.1 680.9 %all-reduce.6.cloned.1.call-start = ((), (), s32[]{:S(2)}) async-start(), calls=%async_computation.4 | async-start | bytes 1769472 | tf_op jit(solution)/shard_map/psum | solution.py:87
  106.3 2.6 copy-start
  194.7 2.6 copy-start.1
Sparse Core Ops, SparseCore 0:
  15.3 90.8 all-gather.6
  111.3 83.3 all-gather.4
  221.0 514.9 all-reduce.5
where the time goes:
time: 747 us; the launch traced here: 746 us
  waiting for transfers between devices  626 us (84%)
  matrix products  58.5 us (8%)
  starting transfers between devices  27.8 us (4%)
  local copies, waits for them, and re-layouts  16.3 us (2%)
  between operations  14.1 us (2%)
    psum x1, waiting for transfers between devices, local(): grad_two, grad_one = lax.psum((grad_two, grad_one), 'dp')  515 us
    all_gather x1, waiting for transfers between devices, local(): lax.all_gather(second_input, 'mp', axis=0, tiled=True)  62.1 us
    dot_general x54, matrix products, fold_taps(): lax.dot_general(tap_grad, flat, (((0,), (0,)), ((), ())), preferred_eleme...  50.8 us
    all_gather x1, waiting for transfers between devices, local(): lax.all_gather(first_in, 'mp', axis=0, tiled=True)  46 us
    all_to_all x2, starting transfers between devices, regroup(): return lax.all_to_all(grad, 'mp', split_axis=3, concat_axis=0, tiled=True)  19.5 us
  transfers between devices with their start and end apart: 7, of which 4 were waited for; matrix products, arithmetic and copies ran while one was open for 6% of the time, Pallas kernels for 0%

commit v1 on v0

v1 whole, which is shorter than its diff:
```python
import jax
import jax.numpy as jnp
from jax import lax
from jax.experimental import pallas as pl
from jax.experimental.pallas import tpu as pltpu
from jax.sharding import Mesh, PartitionSpec as P

F32 = jnp.float32
BF16 = jnp.bfloat16
PLANES = 16
ROWS = 8
COLS = 32
VOX = ROWS * COLS
CHANS = 256
BLK = 64
LINES = 216
PADDED = 224
PIECE = 56

VMEM = pl.BlockSpec(memory_space=pltpu.VMEM)
PARAMS = pltpu.CompilerParams(vmem_limit_bytes=48 * 1024 * 1024)


def shifted(value, step, axis):
    size = value.shape[axis]
    return pltpu.roll(value, (-step) % size, axis)


def spread_kernel(grad_ref, pre_ref, first_ref, out_ref):
    grad = grad_ref[...].reshape(VOX, CHANS).T
    second = jnp.maximum(pre_ref[...].reshape(VOX, CHANS), 0).T
    first = first_ref[...].reshape(VOX, CHANS).T
    for x in range(4):
        for q in range(4):
            dest = x * 4 + q
            out_ref[dest, 0:BLK] = grad[BLK * x : BLK * (x + 1)]
            out_ref[dest, BLK : 2 * BLK] = second[BLK * q : BLK * (q + 1)]
            out_ref[dest, 2 * BLK : 3 * BLK] = first[BLK * q : BLK * (q + 1)]


def spread(grad, pre, first):
    return pl.pallas_call(
        spread_kernel,
        out_shape=jax.ShapeDtypeStruct((PLANES, 3 * BLK, VOX), BF16),
        in_specs=[VMEM] * 3,
        out_specs=VMEM,
        compiler_params=PARAMS,
        name="spread",
    )(grad, pre, first)


def data_grad_kernel(low_ref, own_ref, high_ref, pre_ref, weight_ref, out_ref, held, moved, sems):
    def copy(part):
        columns = pl.ds(part * 3 * CHANS, 3 * CHANS)
        return pltpu.make_async_copy(
            weight_ref.at[:, columns], held.at[part], sems.at[part]
        )

    for part in range(9):
        copy(part).start()
    col = lax.broadcasted_iota(jnp.int32, (VOX, CHANS), 0) % COLS
    blank = jnp.zeros((COLS, CHANS), BF16)
    for a, source in enumerate((high_ref, own_ref, low_ref)):
        plane = source[...].reshape(VOX, CHANS)
        wide = plane.astype(F32)
        views = (
            jnp.where(col < COLS - 1, shifted(wide, 1, 0), 0.0).astype(BF16),
            plane,
            jnp.where(col > 0, shifted(wide, -1, 0), 0.0).astype(BF16),
        )
        for c in range(3):
            moved[a, c, 0:COLS] = blank
            moved[a, c, COLS : COLS + VOX] = views[c]
            moved[a, c, COLS + VOX : 2 * COLS + VOX] = blank
    total = jnp.zeros((VOX, CHANS), F32)
    for a in range(3):
        for b in range(3):
            part = a * 3 + b
            copy(part).wait()
            for c in range(3):
                total = total + jnp.dot(
                    moved[a, c, (2 - b) * COLS : (2 - b) * COLS + VOX],
                    held[part, :, c * CHANS : (c + 1) * CHANS],
                    preferred_element_type=F32,
                )
    pre = pre_ref[...].reshape(VOX, CHANS)
    hidden = jnp.where(pre > 0, total, 0.0).astype(BF16).T
    for x in range(4):
        for q in range(4):
            out_ref[x * 4 + q] = hidden[BLK * x : BLK * (x + 1)]


def data_grad(low, own, high, pre, weight):
    return pl.pallas_call(
        data_grad_kernel,
        out_shape=jax.ShapeDtypeStruct((PLANES, BLK, VOX), BF16),
        in_specs=[VMEM] * 4 + [pl.BlockSpec(memory_space=pl.ANY)],
        out_specs=VMEM,
        scratch_shapes=[
            pltpu.VMEM((9, CHANS, 3 * CHANS), BF16),
            pltpu.VMEM((3, 3, VOX + 2 * COLS, CHANS), BF16),
            pltpu.SemaphoreType.DMA((9,)),
        ],
        compiler_params=PARAMS,
        cost_estimate=pl.CostEstimate(
            flops=2 * VOX * 27 * CHANS * CHANS, bytes_accessed=4 * 1024 * 1024, transcendentals=0
        ),
        name="data_grad",
    )(low, own, high, pre, weight)


def weight_grad_kernel(grad_ref, act_ref, out_ref, grads, acts):
    lane = lax.broadcasted_iota(jnp.int32, (BLK, VOX), 1)
    row, col = lane // COLS, lane % COLS
    for plane in range(PLANES):
        here = slice(plane * VOX, (plane + 1) * VOX)
        act = act_ref[plane]
        wide = act.astype(F32)
        acts[0:BLK, here] = jnp.where(col > 0, shifted(wide, -1, 1), 0.0).astype(BF16)
        acts[BLK : 2 * BLK, here] = act
        acts[2 * BLK : 3 * BLK, here] = jnp.where(
            col < COLS - 1, shifted(wide, 1, 1), 0.0
        ).astype(BF16)
        grad = grad_ref[plane]
        wide = grad.astype(F32)
        views = (
            jnp.where(row < ROWS - 1, shifted(wide, COLS, 1), 0.0).astype(BF16),
            grad,
            jnp.where(row > 0, shifted(wide, -COLS, 1), 0.0).astype(BF16),
        )
        for a in range(3):
            there = plane + a - 1
            if 0 <= there < PLANES:
                for b in range(3):
                    top = (a * 3 + b) * BLK
                    grads[top : top + BLK, there * VOX : (there + 1) * VOX] = views[b]
    blank = jnp.zeros((3 * BLK, VOX), BF16)
    grads[0 : 3 * BLK, (PLANES - 1) * VOX : PLANES * VOX] = blank
    grads[6 * BLK : 9 * BLK, 0:VOX] = blank
    total = lax.dot_general(
        grads[...], acts[...], (((1,), (1,)), ((), ())), preferred_element_type=F32
    )
    for part in range(4):
        pieces = [total[k * BLK + part * 16 : k * BLK + part * 16 + 16] for k in range(9)]
        block = jnp.concatenate(pieces, axis=0)
        out_ref[part, 0:144] = block[:, 0:128].astype(out_ref.dtype)
        tail = block[:, 128:192]
        out_ref[part, 144:LINES] = jnp.concatenate([tail[0:72], tail[72:144]], axis=1).astype(
            out_ref.dtype
        )
        out_ref[part, LINES:PADDED] = jnp.zeros((PADDED - LINES, 128), out_ref.dtype)


def weight_grad(grads, grad_block, acts, act_block):
    return pl.pallas_call(
        weight_grad_kernel,
        out_shape=jax.ShapeDtypeStruct((4, PADDED, 128), F32),
        grid=(1,),
        in_specs=[
            pl.BlockSpec((PLANES, BLK, VOX), lambda i: (0, grad_block, 0)),
            pl.BlockSpec((PLANES, BLK, VOX), lambda i: (0, act_block, 0)),
        ],
        out_specs=pl.BlockSpec((4, PADDED, 128), lambda i: (0, 0, 0)),
        scratch_shapes=[
            pltpu.VMEM((9 * BLK, PLANES * VOX), BF16),
            pltpu.VMEM((3 * BLK, PLANES * VOX), BF16),
        ],
        compiler_params=PARAMS,
        cost_estimate=pl.CostEstimate(
            flops=2 * 27 * BLK * BLK * PLANES * VOX, bytes_accessed=2 * 1024 * 1024, transcendentals=0
        ),
        name="weight_grad",
    )(grads, acts)


def unpack_kernel(lines_ref, out_ref):
    for pair in range(2):
        tiles = [lines_ref[0, 2 * pair + side].astype(F32) for side in range(2)]
        heads = [tile[0:144] for tile in tiles]
        tails = [
            jnp.concatenate([tile[144:LINES, 0:BLK], tile[144:LINES, BLK:128]], axis=0)
            for tile in tiles
        ]
        planes = (
            jnp.concatenate([heads[0][:, 0:BLK], heads[1][:, 0:BLK]], axis=1),
            jnp.concatenate([heads[0][:, BLK:128], heads[1][:, BLK:128]], axis=1),
            jnp.concatenate([tails[0], tails[1]], axis=1),
        )
        for k in range(9):
            for c in range(3):
                start = (3 * k + c) * CHANS + pair * 128
                out_ref[:, start : start + 128] = planes[c][k * 16 : (k + 1) * 16]


def unpack(lines, which):
    return pl.pallas_call(
        unpack_kernel,
        out_shape=jax.ShapeDtypeStruct((16, 27 * CHANS), F32),
        grid=(1,),
        in_specs=[pl.BlockSpec((1, 4, PADDED, 128), lambda i: (which, 0, 0, 0))],
        out_specs=pl.BlockSpec((16, 27 * CHANS), lambda i: (0, 0)),
        compiler_params=PARAMS,
        name="unpack",
    )(lines)


def local(layer_input, hidden_pre, out_grad, weight_second):
    mp = ("x", "yh", "c")
    own = out_grad.reshape(ROWS, COLS, CHANS)
    pre = hidden_pre.reshape(ROWS, COLS, CHANS)
    first = layer_input.reshape(ROWS, COLS, CHANS)
    up = [(i, i + 1) for i in range(PLANES - 1)]
    low = lax.ppermute(own, mp, up)
    high = lax.ppermute(own, mp, [(b, a) for a, b in up])
    given = lax.all_to_all(spread(own, pre, first), mp, 0, 0, tiled=True)
    hidden = data_grad(low, own, high, pre, weight_second)
    hidden = lax.all_to_all(hidden, mp, 0, 0, tiled=True)
    second_part = weight_grad(given, 0, given, 1)
    first_part = weight_grad(hidden, 0, given, 2)
    parts = jnp.stack([second_part, first_part]).reshape(2, 2, 2, 2, 2, PIECE, 128)
    parts = parts.transpose(0, 3, 1, 4, 2, 5, 6).reshape(32, PIECE, 128)
    parts = lax.all_to_all(parts, ("zl", "yh", "yl", "c"), 0, 0, tiled=True)
    mine = parts.reshape(4, 2, 2, 2, PIECE, 128).sum((0, 2)).reshape(4, PIECE, 128)
    sums = lax.all_gather(mine, "zh", axis=0, tiled=False)
    mine = sums.sum(0).astype(BF16)
    lines = jnp.broadcast_to(mine[None], (8, 4, PIECE, 128))
    lines = lax.all_to_all(lines, ("zl", "yl"), 0, 0, tiled=True)
    lines = lines.reshape(2, 4, 4, PIECE, 128).transpose(0, 2, 1, 3, 4).reshape(2, 4, PADDED, 128)
    return unpack(lines, 0), unpack(lines, 1)


def solution(mesh):
    split = Mesh(mesh.devices.reshape(8, 4, 2, 4, 2, 2), ("zh", "zl", "yl", "x", "yh", "c"))
    dp, mp = ("zh", "zl", "yl"), ("x", "yh", "c")
    return jax.shard_map(
        local,
        mesh=split,
        in_specs=(P(dp, mp), P(dp, mp), P(dp, mp), P()),
        out_specs=(P(mp, None), P(mp, None)),
        check_vma=False,
    )
```

time: 747 us -> 174 us (0.23)
  waiting for transfers between devices: 626 us -> 24.5 us
  blocking collectives: 0 us -> 102 us
  matrix products: 58.5 us -> 0 us
  between operations: 14.1 us -> 0.73 us
  local copies, waits for them, and re-layouts: 16.3 us -> 4.89 us
  Pallas kernels: 0 us -> 10.1 us
    psum x1 -> x0, waiting for transfers between devices: 515 us -> none  [local(): grad_two, grad_one = lax.psum((grad_two, grad_one), 'dp')]
    all_gather x2 -> x0, waiting for transfers between devices: 108 us -> none  [the longest x1 62.1 us: local(): lax.all_gather(second_input, 'mp', axis=0, tiled=True)]
    all_gather x0 -> x1, blocking collectives: none -> 60.5 us  [local(): sums = lax.all_gather(mine, 'zh', axis=0, tiled=False)]
    dot_general x81 -> x0, matrix products: 58.5 us -> none  [the longest x54 50.8 us: fold_taps(): lax.dot_general(tap_grad, flat, (((0,), (0,)), ((), ())), preferred_eleme...]
    all_to_all x0 -> x2, blocking collectives: none -> 41.9 us  [the longest x1 26.4 us: local(): parts = lax.all_to_all(parts, ('zl', 'yh', 'yl', 'c'), 0, 0, tiled=True)]
    ppermute x2, waiting for transfers between devices: 0.01 us -> 15.9 us  [the longest x1 13.8 us: local(): high = lax.ppermute(own, mp, [(b, a) for a, b in up])]
    pallas_call x0 -> x6, Pallas kernels: none -> 10.1 us  [the longest x1 3.66 us: data_grad(): pl.pallas_call(data_grad_kernel, out_shape=jax.ShapeDtypeStruct((PLANES,...]
    unnamed x15 -> x12, local copies, waits for them, and re-layouts: 12.5 us -> 4.72 us
  transfers between devices with their start and end apart: 7 -> 4, of which waited for: 4 -> 3; matrix products, arithmetic and copies ran while one was open for 6% -> 0% of each run, Pallas kernels for 0% -> 3%
where the time goes in v1:
time: 174 us; the launch traced here: 173 us
  blocking collectives  102 us (59%)
  starting transfers between devices  29.9 us (17%)
  waiting for transfers between devices  24.5 us (14%)
  Pallas kernels  10.1 us (6%)
  local copies, waits for them, and re-layouts  4.89 us (3%)
    all_gather x1, blocking collectives, local(): sums = lax.all_gather(mine, 'zh', axis=0, tiled=False)  60.5 us
    all_to_all x1, blocking collectives, local(): parts = lax.all_to_all(parts, ('zl', 'yh', 'yl', 'c'), 0, 0, tiled=True)  26.4 us
    all_to_all x1, starting transfers between devices, local(): given = lax.all_to_all(spread(own, pre, first), mp, 0, 0, tiled=True)  16.8 us
    all_to_all x1, blocking collectives, local(): lines = lax.all_to_all(lines, ('zl', 'yl'), 0, 0, tiled=True)  15.5 us
    ppermute x1, waiting for transfers between devices, local(): high = lax.ppermute(own, mp, [(b, a) for a, b in up])  13.8 us
    all_to_all x1, waiting for transfers between devices, local(): hidden = lax.all_to_all(hidden, mp, 0, 0, tiled=True)  8.52 us
    all_to_all x1, starting transfers between devices, local(): hidden = lax.all_to_all(hidden, mp, 0, 0, tiled=True)  6.21 us
    ppermute x1, starting transfers between devices, local(): high = lax.ppermute(own, mp, [(b, a) for a, b in up])  4.91 us
  transfers between devices with their start and end apart: 4, of which 3 were waited for; matrix products, arithmetic and copies ran while one was open for 0% of the time, Pallas kernels for 3%

profile of v1, /device:TPU:6, one launch (start us, length us, event | category | flops | bytes accessed | tf_op | source)
XLA Modules:
  0.0 172.5 jit_solution(1045200849642516500)
XLA Ops:
  0.6 0.0 copy-start.1
  0.6 0.9 copy-done.1
  1.5 0.9 copy-done.3
  2.4 0.9 copy-done.5
  3.3 1.3 spread.1
  4.7 16.8 %all-to-all-start = ((bf16[16,192,256]{2,1,0:T(8,128)(2,1)}), bf16[16,192,256]{2,1,0:T(8,128)(2,1)S(1)}, u32[]{:S(2)}, u32[]{:S(2)}) async-start(bf16[16,192,256]{2,1,0:T(8,128)(2,1)} %spread.1), calls=%async_computation | async-start | bytes 3145728 | tf_op jit(solution)/shard_map/all_to_all | solution.py:215
  21.5 4.9 %collective-permute-start.1 = (bf16[8,32,256]{2,1,0:T(8,128)(2,1)S(1)}, bf16[8,32,256]{2,1,0:T(8,128)(2,1)S(1)}, u32[]{:S(2)}, u32[]{:S(2)}) collective-permute-start(bf16[8,32,256]{2,1,0:T(8,128)(2,1)S(1)} %bitcast.18), channel_id=1, source_target_pairs={{1,0},{2,1},{3,2},{4,3},{5,4},{6,5},{7,6},{8,7},{9,8},{10,9},{11,1... | collective-permute-start | bytes 393224 | tf_op jit(solution)/shard_map/ppermute | solution.py:214
  26.4 1.9 %collective-permute-start = (bf16[8,32,256]{2,1,0:T(8,128)(2,1)S(1)}, bf16[8,32,256]{2,1,0:T(8,128)(2,1)S(1)}, u32[]{:S(2)}, u32[]{:S(2)}) collective-permute-start(bf16[8,32,256]{2,1,0:T(8,128)(2,1)S(1)} %bitcast.19), channel_id=1, source_target_pairs={{0,1},{1,2},{2,3},{3,4},{4,5},{5,6},{6,7},{7,8},{8,9},{9,10},{10,1... | collective-permute-start | bytes 393224 | tf_op jit(solution)/shard_map/ppermute | solution.py:213
  28.4 13.8 %collective-permute-done.1.high_ref = bf16[8,32,256]{2,1,0:T(8,128)(2,1)S(1)} collective-permute-done((bf16[8,32,256]{2,1,0:T(8,128)(2,1)S(1)}, bf16[8,32,256]{2,1,0:T(8,128)(2,1)S(1)}, u32[]{:S(2)}, u32[]{:S(2)}) %collective-permute-start.1) | collective-permute-done | bytes 131104 | tf_op jit(solution)/shard_map/ppermute | solution.py:214
  42.2 2.1 %collective-permute-done.low_ref = bf16[8,32,256]{2,1,0:T(8,128)(2,1)S(1)} collective-permute-done((bf16[8,32,256]{2,1,0:T(8,128)(2,1)S(1)}, bf16[8,32,256]{2,1,0:T(8,128)(2,1)S(1)}, u32[]{:S(2)}, u32[]{:S(2)}) %collective-permute-start) | collective-permute-done | bytes 131104 | tf_op jit(solution)/shard_map/ppermute | solution.py:213
  44.3 2.0 %copy-done = bf16[256,6912]{1,0:T(8,128)(2,1)S(1)} copy-done((bf16[256,6912]{1,0:T(8,128)(2,1)S(1)}, bf16[256,6912]{1,0:T(8,128)(2,1)}, u32[]{:S(2)}) %copy-start) | copy-done | bytes 3538968
  46.3 3.7 %data_grad.1 = bf16[16,64,256]{2,1,0:T(8,128)(2,1)} custom-call(bf16[8,32,256]{2,1,0:T(8,128)(2,1)S(1)} %collective-permute-done.low_ref, bf16[8,32,256]{2,1,0:T(8,128)(2,1)S(1)} %bitcast.20, bf16[8,32,256]{2,1,0:T(8,128)(2,1)S(1)} %collective-permute-done.1.high_ref, bf16[8,32,256]{2,1,0:T(8,128)(2,1)S(1)} %bitcast.22, bf16[256,6912]{1,0:T(8,128)(2,1)S(1)} %copy-done), custom_call_target="tpu_custom_call" | custom-call | flops 905969664 | bytes 4194304 | tf_op jit(solution)/shard_map/data_grad/pallas_call | solution.py:94
  50.0 6.2 %all-to-all-start.1 = ((bf16[16,64,256]{2,1,0:T(8,128)(2,1)}), bf16[16,64,256]{2,1,0:T(8,128)(2,1)S(1)}, u32[]{:S(2)}, u32[]{:S(2)}) async-start(bf16[16,64,256]{2,1,0:T(8,128)(2,1)} %data_grad.1), calls=%async_computation.1 | async-start | bytes 1048576 | tf_op jit(solution)/shard_map/all_to_all | solution.py:217
  56.2 1.6 weight_grad.2
  57.8 8.5 %all-to-all-done.1.grad_ref = bf16[16,64,256]{2,1,0:T(8,128)(2,1)S(1)} async-done(((bf16[16,64,256]{2,1,0:T(8,128)(2,1)}), bf16[16,64,256]{2,1,0:T(8,128)(2,1)S(1)}, u32[]{:S(2)}, u32[]{:S(2)}) %all-to-all-start.1) | async-done | bytes 524320 | tf_op jit(solution)/shard_map/all_to_all | solution.py:217
  66.3 1.6 weight_grad.3
  67.8 0.1 pad_maximum_fusion
  67.9 0.1 copy.12
  68.0 26.4 %all_to_all.20 = f32[32,56,128]{2,1,0:T(8,128)S(1)} all-to-all(f32[32,56,128]{2,1,0:T(8,128)S(1)} %bitcast.25), channel_id=1, replica_groups=mesh['zh'=8,'zl'=4,'yl'=2,'x'=4,'yh'=2,'c'=2] {'zl','yh','yl','c'}, dimensions={0} | all-to-all | bytes 1835008 | tf_op jit(solution)/shard_map/all_to_all | solution.py:222
  94.5 60.5 %all_gather.3 = f32[8,4,56,128]{3,2,1,0:T(8,128)S(1)} all-gather(f32[1,4,56,128]{3,2,1,0:T(8,128)S(1)} %bitcast.28), channel_id=1, replica_groups=mesh['zh'=8,'zl'=4,'yl'=2,'x'=4,'yh'=2,'c'=2] {'zh'}, dimensions={0}, use_global_device_ids=true | all-gather | bytes 1032192 | tf_op jit(solution)/shard_map/all_gather | solution.py:224
  155.0 0.1 broadcast_in_dim.2
  155.1 15.5 %all_to_all.21 = bf16[8,4,56,128]{3,2,1,0:T(8,128)(2,1)S(1)} all-to-all(bf16[8,4,56,128]{3,2,1,0:T(8,128)(2,1)S(1)} %broadcast_in_dim.2), channel_id=1, replica_groups=mesh['zh'=8,'zl'=4,'yl'=2,'x'=4,'yh'=2,'c'=2] {'zl','yl'}, dimensions={0} | all-to-all | bytes 917504 | tf_op jit(solution)/shard_map/all_to_all | solution.py:227
  170.6 1.0 unpack.3
  171.6 1.0 unpack.2
  (11 shorter events, 0.2 us)
Async XLA Ops:
  0.6 0.9 copy-start.1
  1.5 0.9 copy-start.3
  2.4 0.9 copy-start.5
  4.7 16.8 %copy-start.2 = (bf16[1,1,8,32,256]{4,3,2,1,0:T(8,128)(2,1)S(1)}, bf16[1,1,8,32,256]{4,3,2,1,0:T(8,128)(2,1)}, u32[]{:S(2)}) copy-start(bf16[1,1,8,32,256]{4,3,2,1,0:T(8,128)(2,1)} %param.6) | copy-start | bytes 393220
  4.7 39.6 %copy-start.4 = (bf16[1,1,8,32,256]{4,3,2,1,0:T(8,128)(2,1)S(1)}, bf16[1,1,8,32,256]{4,3,2,1,0:T(8,128)(2,1)}, u32[]{:S(2)}) copy-start(bf16[1,1,8,32,256]{4,3,2,1,0:T(8,128)(2,1)} %param.5) | copy-start | bytes 393220
  4.7 45.3 %all-to-all-start = ((bf16[16,192,256]{2,1,0:T(8,128)(2,1)}), bf16[16,192,256]{2,1,0:T(8,128)(2,1)S(1)}, u32[]{:S(2)}, u32[]{:S(2)}) async-start(bf16[16,192,256]{2,1,0:T(8,128)(2,1)} %spread.1), calls=%async_computation | async-start | bytes 3145728 | tf_op jit(solution)/shard_map/all_to_all | solution.py:215
  21.5 20.7 %collective-permute-start.1 = (bf16[8,32,256]{2,1,0:T(8,128)(2,1)S(1)}, bf16[8,32,256]{2,1,0:T(8,128)(2,1)S(1)}, u32[]{:S(2)}, u32[]{:S(2)}) collective-permute-start(bf16[8,32,256]{2,1,0:T(8,128)(2,1)S(1)} %bitcast.18), channel_id=1, source_target_pairs={{1,0},{2,1},{3,2},{4,3},{5,4},{6,5},{7,6},{8,7},{9,8},{10,9},{11,1... | collective-permute-start | bytes 393224 | tf_op jit(solution)/shard_map/ppermute | solution.py:214
  26.4 17.9 %collective-permute-start = (bf16[8,32,256]{2,1,0:T(8,128)(2,1)S(1)}, bf16[8,32,256]{2,1,0:T(8,128)(2,1)S(1)}, u32[]{:S(2)}, u32[]{:S(2)}) collective-permute-start(bf16[8,32,256]{2,1,0:T(8,128)(2,1)S(1)} %bitcast.19), channel_id=1, source_target_pairs={{0,1},{1,2},{2,3},{3,4},{4,5},{5,6},{6,7},{7,8},{8,9},{9,10},{10,1... | collective-permute-start | bytes 393224 | tf_op jit(solution)/shard_map/ppermute | solution.py:213
  44.3 2.0 %copy-start = (bf16[256,6912]{1,0:T(8,128)(2,1)S(1)}, bf16[256,6912]{1,0:T(8,128)(2,1)}, u32[]{:S(2)}) copy-start(bf16[256,6912]{1,0:T(8,128)(2,1)} %weight_ref.1) | copy-start | bytes 10616836
  50.0 16.3 %all-to-all-start.1 = ((bf16[16,64,256]{2,1,0:T(8,128)(2,1)}), bf16[16,64,256]{2,1,0:T(8,128)(2,1)S(1)}, u32[]{:S(2)}, u32[]{:S(2)}) async-start(bf16[16,64,256]{2,1,0:T(8,128)(2,1)} %data_grad.1), calls=%async_computation.1 | async-start | bytes 1048576 | tf_op jit(solution)/shard_map/all_to_all | solution.py:217

commit v2 on v1

v2 whole, which is shorter than its diff:
```python
import jax
import jax.numpy as jnp
from jax import lax
from jax.experimental import pallas as pl
from jax.experimental.pallas import tpu as pltpu
from jax.sharding import Mesh, PartitionSpec as P

F32 = jnp.float32
BF16 = jnp.bfloat16
F16 = jnp.float16
PLANES = 16
ROWS = 8
COLS = 32
VOX = ROWS * COLS
CHANS = 256
BLK = 64
LINES = 216
DATA = 54
PIECE = 56
TOP = 14.0

VMEM = pl.BlockSpec(memory_space=pltpu.VMEM)
PARAMS = pltpu.CompilerParams(vmem_limit_bytes=48 * 1024 * 1024)


def shifted(value, step, axis):
    size = value.shape[axis]
    return pltpu.roll(value, (-step) % size, axis)


def front_kernel(
    low_ref, own_ref, high_ref, pre_ref, first_ref, weight_ref, out_ref, held, moved, sems
):
    def copy(part):
        columns = pl.ds(part * 3 * CHANS, 3 * CHANS)
        return pltpu.make_async_copy(
            weight_ref.at[:, columns], held.at[part], sems.at[part]
        )

    for part in range(9):
        copy(part).start()
    col = lax.broadcasted_iota(jnp.int32, (VOX, CHANS), 0) % COLS
    blank = jnp.zeros((COLS, CHANS), BF16)
    for a, source in enumerate((high_ref, own_ref, low_ref)):
        plane = source[...].reshape(VOX, CHANS)
        wide = plane.astype(F32)
        views = (
            jnp.where(col < COLS - 1, shifted(wide, 1, 0), 0.0).astype(BF16),
            plane,
            jnp.where(col > 0, shifted(wide, -1, 0), 0.0).astype(BF16),
        )
        for c in range(3):
            moved[a, c, 0:COLS] = blank
            moved[a, c, COLS : COLS + VOX] = views[c]
            moved[a, c, COLS + VOX : 2 * COLS + VOX] = blank
    total = jnp.zeros((VOX, CHANS), F32)
    for a in range(3):
        for b in range(3):
            part = a * 3 + b
            copy(part).wait()
            for c in range(3):
                total = total + jnp.dot(
                    moved[a, c, (2 - b) * COLS : (2 - b) * COLS + VOX],
                    held[part, :, c * CHANS : (c + 1) * CHANS],
                    preferred_element_type=F32,
                )
    pre = pre_ref[...].reshape(VOX, CHANS)
    hidden = jnp.where(pre > 0, total, 0.0).astype(BF16).T
    grad = own_ref[...].reshape(VOX, CHANS).T
    second = jnp.maximum(pre, 0).T
    first = first_ref[...].reshape(VOX, CHANS).T
    for x in range(4):
        for q in range(4):
            dest = x * 4 + q
            out_ref[dest, 0:BLK] = grad[BLK * x : BLK * (x + 1)]
            out_ref[dest, BLK : 2 * BLK] = second[BLK * q : BLK * (q + 1)]
            out_ref[dest, 2 * BLK : 3 * BLK] = hidden[BLK * x : BLK * (x + 1)]
            out_ref[dest, 3 * BLK : 4 * BLK] = first[BLK * q : BLK * (q + 1)]


def front(low, own, high, pre, first, weight):
    return pl.pallas_call(
        front_kernel,
        out_shape=jax.ShapeDtypeStruct((PLANES, 4 * BLK, VOX), BF16),
        in_specs=[VMEM] * 5 + [pl.BlockSpec(memory_space=pltpu.HBM)],
        out_specs=VMEM,
        scratch_shapes=[
            pltpu.VMEM((9, CHANS, 3 * CHANS), BF16),
            pltpu.VMEM((3, 3, VOX + 2 * COLS, CHANS), BF16),
            pltpu.SemaphoreType.DMA((9,)),
        ],
        compiler_params=PARAMS,
        cost_estimate=pl.CostEstimate(
            flops=2 * VOX * 27 * CHANS * CHANS, bytes_accessed=4 * 1024 * 1024, transcendentals=0
        ),
        name="front",
    )(low, own, high, pre, first, weight)


def weight_grad_kernel(grad_ref, act_ref, out_ref, grads, acts):
    lane = lax.broadcasted_iota(jnp.int32, (BLK, VOX), 1)
    row, col = lane // COLS, lane % COLS
    for plane in range(PLANES):
        here = slice(plane * VOX, (plane + 1) * VOX)
        act = act_ref[plane]
        wide = act.astype(F32)
        acts[0:BLK, here] = jnp.where(col > 0, shifted(wide, -1, 1), 0.0).astype(BF16)
        acts[BLK : 2 * BLK, here] = act
        acts[2 * BLK : 3 * BLK, here] = jnp.where(
            col < COLS - 1, shifted(wide, 1, 1), 0.0
        ).astype(BF16)
        grad = grad_ref[plane]
        wide = grad.astype(F32)
        views = (
            jnp.where(row < ROWS - 1, shifted(wide, COLS, 1), 0.0).astype(BF16),
            grad,
            jnp.where(row > 0, shifted(wide, -COLS, 1), 0.0).astype(BF16),
        )
        for a in range(3):
            there = plane + a - 1
            if 0 <= there < PLANES:
                for b in range(3):
                    top = (a * 3 + b) * BLK
                    grads[top : top + BLK, there * VOX : (there + 1) * VOX] = views[b]
    blank = jnp.zeros((3 * BLK, VOX), BF16)
    grads[0 : 3 * BLK, (PLANES - 1) * VOX : PLANES * VOX] = blank
    grads[6 * BLK : 9 * BLK, 0:VOX] = blank
    total = lax.dot_general(
        grads[...], acts[...], (((1,), (1,)), ((), ())), preferred_element_type=F32
    )
    peak = jnp.max(jnp.abs(total), axis=0, keepdims=True)
    peak = jnp.max(peak, axis=1, keepdims=True)
    power = jnp.ceil(jnp.log2(jnp.maximum(peak, 2.0**-100)))
    total = total * jnp.exp2(TOP - power)
    tag = jnp.broadcast_to(power, (PIECE - DATA, 128))
    for part in range(4):
        pieces = [total[k * BLK + part * 16 : k * BLK + part * 16 + 16] for k in range(9)]
        block = jnp.concatenate(pieces, axis=0)
        tail = block[:, 128:192]
        tail = jnp.concatenate([tail[0:72], tail[72:144]], axis=1)
        lines = jnp.concatenate([block[:, 0:128], tail], axis=0)
        for half in range(2):
            for yl in range(2):
                start = (half * 2 + yl) * DATA
                dest = ((half * 2 + part // 2) * 2 + yl) * 2 + part % 2
                out_ref[dest] = jnp.concatenate([lines[start : start + DATA], tag], axis=0)


def weight_grads(given):
    return pl.pallas_call(
        weight_grad_kernel,
        out_shape=jax.ShapeDtypeStruct((32, PIECE, 128), F32),
        grid=(2,),
        in_specs=[
            pl.BlockSpec((PLANES, BLK, VOX), lambda i: (0, 2 * i, 0)),
            pl.BlockSpec((PLANES, BLK, VOX), lambda i: (0, 2 * i + 1, 0)),
        ],
        out_specs=pl.BlockSpec((16, PIECE, 128), lambda i: (i, 0, 0)),
        scratch_shapes=[
            pltpu.VMEM((9 * BLK, PLANES * VOX), BF16),
            pltpu.VMEM((3 * BLK, PLANES * VOX), BF16),
        ],
        compiler_params=PARAMS,
        cost_estimate=pl.CostEstimate(
            flops=4 * 27 * BLK * BLK * PLANES * VOX, bytes_accessed=4 * 1024 * 1024, transcendentals=0
        ),
        name="weight_grads",
    )(given, given)


def merge_kernel(parts_ref, out_ref):
    tags = [parts_ref[source, DATA : DATA + 1, 0:1] for source in range(32)]
    peak = tags[0]
    for tag in tags[1:]:
        peak = jnp.maximum(peak, tag)
    peak = peak + 3.0
    line = lax.broadcasted_iota(jnp.int32, (PIECE, 128), 0)
    for q in range(4):
        sources = [zl * 8 + (q // 2) * 4 + yl * 2 + q % 2 for zl in range(4) for yl in range(2)]
        total = jnp.zeros((PIECE, 128), F32)
        for source in sources:
            total = total + parts_ref[source] * jnp.exp2(tags[source] - peak)
        out_ref[q * PIECE : (q + 1) * PIECE] = jnp.where(line < DATA, total, peak)


def merge(parts):
    return pl.pallas_call(
        merge_kernel,
        out_shape=jax.ShapeDtypeStruct((4 * PIECE, 128), F32),
        in_specs=[VMEM],
        out_specs=VMEM,
        compiler_params=PARAMS,
        name="merge",
    )(parts)


def finish_kernel(sums_ref, out_ref):
    scales = [jnp.exp2(sums_ref[z, DATA : DATA + 1, 0:1] - TOP) for z in range(8)]
    for q in range(4):
        total = jnp.zeros((PIECE, 128), F32)
        for z in range(8):
            total = total + sums_ref[z, q * PIECE : (q + 1) * PIECE] * scales[z]
        total = total.astype(BF16)
        for dest in range(8):
            out_ref[dest, q] = total


def finish(sums):
    return pl.pallas_call(
        finish_kernel,
        out_shape=jax.ShapeDtypeStruct((8, 4, PIECE, 128), BF16),
        in_specs=[VMEM],
        out_specs=VMEM,
        compiler_params=PARAMS,
        name="finish",
    )(sums)


def unpack_kernel(pieces_ref, *out_refs):
    for which, out_ref in enumerate(out_refs):
        for pair in range(2):
            tiles = [
                jnp.concatenate(
                    [
                        pieces_ref[which * 4 + piece, 2 * pair + side].astype(F32)[0:DATA]
                        for piece in range(4)
                    ],
                    axis=0,
                )
                for side in range(2)
            ]
            tails = [
                jnp.concatenate([tile[144:LINES, 0:BLK], tile[144:LINES, BLK:128]], axis=0)
                for tile in tiles
            ]
            planes = (
                jnp.concatenate([tile[0:144, 0:BLK] for tile in tiles], axis=1),
                jnp.concatenate([tile[0:144, BLK:128] for tile in tiles], axis=1),
                jnp.concatenate(tails, axis=1),
            )
            for k in range(9):
                for c in range(3):
                    start = (3 * k + c) * CHANS + pair * 128
                    out_ref[:, start : start + 128] = planes[c][k * 16 : (k + 1) * 16]


def unpack(pieces):
    return pl.pallas_call(
        unpack_kernel,
        out_shape=[jax.ShapeDtypeStruct((16, 27 * CHANS), F32)] * 2,
        in_specs=[VMEM],
        out_specs=[VMEM] * 2,
        compiler_params=PARAMS,
        name="unpack",
    )(pieces)


def local(layer_input, hidden_pre, out_grad, weight_second):
    mp = ("x", "yh", "c")
    own = out_grad.reshape(ROWS, COLS, CHANS)
    pre = hidden_pre.reshape(ROWS, COLS, CHANS)
    first = layer_input.reshape(ROWS, COLS, CHANS)
    up = [(i, i + 1) for i in range(PLANES - 1)]
    low = lax.ppermute(own, mp, up)
    high = lax.ppermute(own, mp, [(b, a) for a, b in up])
    given = lax.all_to_all(
        front(low, own, high, pre, first, weight_second), mp, 0, 0, tiled=True
    )
    parts = weight_grads(given).astype(F16)
    parts = lax.all_to_all(parts, ("zl", "yh", "yl", "c"), 0, 0, tiled=True)
    mine = merge(parts.astype(F32)).astype(F16)
    sums = lax.all_gather(mine, "zh", axis=0, tiled=True).reshape(8, 4 * PIECE, 128)
    pieces = lax.all_to_all(finish(sums.astype(F32)), ("zl", "yl"), 0, 0, tiled=True)
    return tuple(unpack(pieces))


def solution(mesh):
    split = Mesh(mesh.devices.reshape(8, 4, 2, 4, 2, 2), ("zh", "zl", "yl", "x", "yh", "c"))
    dp, mp = ("zh", "zl", "yl"), ("x", "yh", "c")
    return jax.shard_map(
        local,
        mesh=split,
        in_specs=(P(dp, mp), P(dp, mp), P(dp, mp), P()),
        out_specs=(P(mp, None), P(mp, None)),
        check_vma=False,
    )
```

time: 174 us -> 146 us (0.84)
  starting transfers between devices: 29.9 us -> 6.73 us
  waiting for transfers between devices: 24.5 us -> 6.97 us
  blocking collectives: 102 us -> 119 us
  local copies, waits for them, and re-layouts: 4.89 us -> 2.71 us
    all_to_all x1 -> x2, blocking collectives: 15.5 us -> 50.1 us  [the longest x1 37.8 us: local(): lax.all_to_all(front(low, own, high, pre, first, weight_second), mp, 0, 0...]
    all_to_all x2 -> x0, starting transfers between devices: 23 us -> none  [the longest x1 16.8 us: local(): given = lax.all_to_all(spread(own, pre, first), mp, 0, 0, tiled=True)]
    ppermute x1, waiting for transfers between devices: 13.8 us -> 0.89 us  [local(): high = lax.ppermute(own, mp, [(b, a) for a, b in up])]
    all_gather x1, blocking collectives: 60.5 us -> 50.9 us  [local(): lax.all_gather(mine, 'zh', axis=0, tiled=True).reshape(8, 4 * PIECE, 128)]
    all_to_all x1, blocking collectives: 26.4 us -> 17.7 us  [local(): parts = lax.all_to_all(parts, ('zl', 'yh', 'yl', 'c'), 0, 0, tiled=True)]
    all_to_all x2 -> x0, waiting for transfers between devices: 8.52 us -> none  [the longest x1 8.52 us: local(): hidden = lax.all_to_all(hidden, mp, 0, 0, tiled=True)]
    ppermute x1, waiting for transfers between devices: 2.14 us -> 6.08 us  [local(): low = lax.ppermute(own, mp, up)]
    unnamed x12 -> x6, local copies, waits for them, and re-layouts: 4.72 us -> 2.71 us
  transfers between devices with their start and end apart: 4 -> 2, of which waited for: 3 -> 2; matrix products, arithmetic and copies ran while one was open for 0% -> 0% of each run, Pallas kernels for 3% -> 0%
where the time goes in v2:
time: 146 us; the launch traced here: 144 us
  blocking collectives  119 us (82%)
  Pallas kernels  8.47 us (6%)
  waiting for transfers between devices  6.97 us (5%)
  starting transfers between devices  6.73 us (5%)
  local copies, waits for them, and re-layouts  2.71 us (2%)
    all_gather x1, blocking collectives, local(): lax.all_gather(mine, 'zh', axis=0, tiled=True).reshape(8, 4 * PIECE, 128)  50.9 us
    all_to_all x1, blocking collectives, local(): lax.all_to_all(front(low, own, high, pre, first, weight_second), mp, 0, 0...  37.8 us
    all_to_all x1, blocking collectives, local(): parts = lax.all_to_all(parts, ('zl', 'yh', 'yl', 'c'), 0, 0, tiled=True)  17.7 us
    all_to_all x1, blocking collectives, local(): lax.all_to_all(finish(sums.astype(F32)), ('zl', 'yl'), 0, 0, tiled=True)  12.3 us
    ppermute x1, waiting for transfers between devices, local(): low = lax.ppermute(own, mp, up)  6.08 us
    ppermute x1, starting transfers between devices, local(): high = lax.ppermute(own, mp, [(b, a) for a, b in up])  4.81 us
    pallas_call x1, Pallas kernels, weight_grads(): pl.pallas_call(weight_grad_kernel, out_shape=jax.ShapeDtypeStruct((32, PI...  3.63 us
    pallas_call x1, Pallas kernels, front(): pl.pallas_call(front_kernel, out_shape=jax.ShapeDtypeStruct((PLANES, 4 *...  3.45 us
  transfers between devices with their start and end apart: 2, of which 2 were waited for; matrix products, arithmetic and copies ran while one was open for 0% of the time, Pallas kernels for 0%

profile of v2, /device:TPU:6, one launch (start us, length us, event | category | flops | bytes accessed | tf_op | source)
XLA Modules:
  0.0 144.4 jit_solution(13953004208094458103)
XLA Ops:
  0.6 4.8 %collective-permute-start.1 = (bf16[8,32,256]{2,1,0:T(8,128)(2,1)}, bf16[8,32,256]{2,1,0:T(8,128)(2,1)S(1)}, u32[]{:S(2)}, u32[]{:S(2)}) collective-permute-start(bf16[8,32,256]{2,1,0:T(8,128)(2,1)} %bitcast.5), channel_id=1, source_target_pairs={{1,0},{2,1},{3,2},{4,3},{5,4},{6,5},{7,6},{8,7},{9,8},{10,9},{11,1... | collective-permute-start | bytes 393224 | tf_op jit(solution)/shard_map/ppermute | solution.py:265
  5.4 1.9 %collective-permute-start = (bf16[8,32,256]{2,1,0:T(8,128)(2,1)}, bf16[8,32,256]{2,1,0:T(8,128)(2,1)S(1)}, u32[]{:S(2)}, u32[]{:S(2)}) collective-permute-start(bf16[8,32,256]{2,1,0:T(8,128)(2,1)} %bitcast.6), channel_id=1, source_target_pairs={{0,1},{1,2},{2,3},{3,4},{4,5},{5,6},{6,7},{7,8},{8,9},{9,10},{10,1... | collective-permute-start | bytes 393224 | tf_op jit(solution)/shard_map/ppermute | solution.py:264
  7.4 0.9 collective-permute-done.1.high_ref
  8.3 6.1 %collective-permute-done.low_ref = bf16[8,32,256]{2,1,0:T(8,128)(2,1)S(1)} collective-permute-done((bf16[8,32,256]{2,1,0:T(8,128)(2,1)}, bf16[8,32,256]{2,1,0:T(8,128)(2,1)S(1)}, u32[]{:S(2)}, u32[]{:S(2)}) %collective-permute-start) | collective-permute-done | bytes 131104 | tf_op jit(solution)/shard_map/ppermute | solution.py:264
  14.3 0.0 copy-start
  14.3 0.9 copy-done
  15.3 0.0 copy-start.1
  15.3 0.9 copy-done.1
  16.2 0.0 copy-start.2
  16.2 0.9 copy-done.2
  17.1 3.5 %front.1 = bf16[16,256,256]{2,1,0:T(8,128)(2,1)S(1)} custom-call(bf16[8,32,256]{2,1,0:T(8,128)(2,1)S(1)} %collective-permute-done.low_ref, bf16[8,32,256]{2,1,0:T(8,128)(2,1)S(1)} %bitcast.7, bf16[8,32,256]{2,1,0:T(8,128)(2,1)S(1)} %collective-permute-done.1.high_ref, bf16[8,32,256]{2,1,0:T(8,128)(2,1)S(1)} %bitcast.8, bf16[8,32,256]{2,1,0:T(8,128)(2,1)S(1)} %bitcast.9, ...), custom_call_target="tpu_custom_call" | custom-call | flops 905969664 | bytes 4194304 | tf_op jit(solution)/shard_map/front/pallas_call | solution.py:82
  20.5 37.8 %all_to_all.15.grad_ref.act_ref = bf16[16,256,256]{2,1,0:T(8,128)(2,1)S(1)} all-to-all(bf16[16,256,256]{2,1,0:T(8,128)(2,1)S(1)} %front.1), channel_id=1, replica_groups=mesh['zh'=8,'zl'=4,'yl'=2,'x'=4,'yh'=2,'c'=2] {'x','yh','c'}, dimensions={0} | all-to-all | bytes 4194304 | tf_op jit(solution)/shard_map/all_to_all | solution.py:266
  58.3 3.6 %weight_grads.1 = f32[32,56,128]{2,1,0:T(8,128)S(1)} custom-call(bf16[16,256,256]{2,1,0:T(8,128)(2,1)S(1)} %all_to_all.15.grad_ref.act_ref, bf16[16,256,256]{2,1,0:T(8,128)(2,1)S(1)} %all_to_all.15.grad_ref.act_ref), custom_call_target="tpu_custom_call" | custom-call | flops 1811939328 | bytes 4194304 | tf_op jit(solution)/shard_map/weight_grads/pallas_call | solution.py:150
  61.9 0.1 convert_element_type.14
  62.0 17.7 %all_to_all.16 = f16[32,56,128]{2,1,0:T(8,128)(2,1)S(1)} all-to-all(f16[32,56,128]{2,1,0:T(8,128)(2,1)S(1)} %convert_element_type.14), channel_id=1, replica_groups=mesh['zh'=8,'zl'=4,'yl'=2,'x'=4,'yh'=2,'c'=2] {'zl','yh','yl','c'}, dimensions={0} | all-to-all | bytes 917504 | tf_op jit(solution)/shard_map/all_to_all | solution.py:270
  79.7 0.1 convert_element_type.15.parts_ref
  79.7 0.1 merge.1
  79.9 50.9 %all_gather.3 = f16[1792,128]{1,0:T(8,128)(2,1)S(1)} all-gather(f16[224,128]{1,0:T(8,128)(2,1)S(1)} %convert_element_type.16), channel_id=1, replica_groups=mesh['zh'=8,'zl'=4,'yl'=2,'x'=4,'yh'=2,'c'=2] {'zh'}, dimensions={0}, use_global_device_ids=true | all-gather | bytes 516096 | tf_op jit(solution)/shard_map/all_gather | solution.py:272
  130.8 0.1 convert.1.sums_ref
  130.8 0.1 finish.1
  131.0 12.3 %all_to_all.17.pieces_ref = bf16[8,4,56,128]{3,2,1,0:T(8,128)(2,1)S(1)} all-to-all(bf16[8,4,56,128]{3,2,1,0:T(8,128)(2,1)S(1)} %finish.1), channel_id=1, replica_groups=mesh['zh'=8,'zl'=4,'yl'=2,'x'=4,'yh'=2,'c'=2] {'zl','yl'}, dimensions={0} | all-to-all | bytes 917504 | tf_op jit(solution)/shard_map/all_to_all | solution.py:273
  143.3 1.1 unpack.1
  (1 shorter events, 0.0 us)
Async XLA Ops:
  0.6 7.6 %collective-permute-start.1 = (bf16[8,32,256]{2,1,0:T(8,128)(2,1)}, bf16[8,32,256]{2,1,0:T(8,128)(2,1)S(1)}, u32[]{:S(2)}, u32[]{:S(2)}) collective-permute-start(bf16[8,32,256]{2,1,0:T(8,128)(2,1)} %bitcast.5), channel_id=1, source_target_pairs={{1,0},{2,1},{3,2},{4,3},{5,4},{6,5},{7,6},{8,7},{9,8},{10,9},{11,1... | collective-permute-start | bytes 393224 | tf_op jit(solution)/shard_map/ppermute | solution.py:265
  5.4 8.9 %collective-permute-start = (bf16[8,32,256]{2,1,0:T(8,128)(2,1)}, bf16[8,32,256]{2,1,0:T(8,128)(2,1)S(1)}, u32[]{:S(2)}, u32[]{:S(2)}) collective-permute-start(bf16[8,32,256]{2,1,0:T(8,128)(2,1)} %bitcast.6), channel_id=1, source_target_pairs={{0,1},{1,2},{2,3},{3,4},{4,5},{5,6},{6,7},{7,8},{8,9},{9,10},{10,1... | collective-permute-start | bytes 393224 | tf_op jit(solution)/shard_map/ppermute | solution.py:264
  14.3 0.9 copy-start
  15.3 0.9 copy-start.1
  16.2 0.9 copy-start.2

commit v3 on v2

v3 whole, which is shorter than its diff:
```python
import jax
import jax.numpy as jnp
from jax import lax
from jax.experimental import pallas as pl
from jax.experimental.pallas import tpu as pltpu
from jax.sharding import Mesh, PartitionSpec as P

F32 = jnp.float32
BF16 = jnp.bfloat16
F16 = jnp.float16
PLANES = 16
ROWS = 8
COLS = 32
VOX = ROWS * COLS
CHANS = 256
OUTS = 64
INS = 128
DATA = 54
PIECE = 56
TOP = 14.0

VMEM = pl.BlockSpec(memory_space=pltpu.VMEM)
PARAMS = pltpu.CompilerParams(vmem_limit_bytes=48 * 1024 * 1024)


def shifted(value, step, axis):
    size = value.shape[axis]
    return pltpu.roll(value, (-step) % size, axis)


def fill_views(plane, moved):
    col = lax.broadcasted_iota(jnp.int32, (VOX, CHANS), 0) % COLS
    blank = jnp.zeros((COLS, CHANS), BF16)
    wide = plane.astype(F32)
    views = (
        jnp.where(col < COLS - 1, shifted(wide, 1, 0), 0.0).astype(BF16),
        plane,
        jnp.where(col > 0, shifted(wide, -1, 0), 0.0).astype(BF16),
    )
    for c in range(3):
        moved[c, 0:COLS] = blank
        moved[c, COLS : COLS + VOX] = views[c]
        moved[c, COLS + VOX : 2 * COLS + VOX] = blank


def row_taps(total, moved, b, weight):
    start = (2 - b) * COLS
    for c in range(3):
        total = total + jnp.dot(
            moved[c, start : start + VOX],
            weight[:, c * CHANS : (c + 1) * CHANS],
            preferred_element_type=F32,
        )
    return total


def early_kernel(
    own_ref, pre_ref, first_ref, weight_ref, part_ref, kept_ref, turned_ref,
    planes, held, moved, plane_sems, held_sems, kept_sems,
):
    loads = [
        pltpu.make_async_copy(ref, planes.at[k], plane_sems.at[k])
        for k, ref in enumerate((own_ref, pre_ref, first_ref))
    ]

    def weights(part, target, sem):
        columns = pl.ds(part * 3 * CHANS, 3 * CHANS)
        return pltpu.make_async_copy(weight_ref.at[:, columns], target, sem)

    centre = [weights(3 + k, held.at[k], held_sems.at[k]) for k in range(3)]
    outer = [
        weights(part, kept_ref.at[k], kept_sems.at[k]) for k, part in enumerate((0, 1, 2, 6, 7, 8))
    ]
    for copy in loads + centre + outer:
        copy.start()
    loads[0].wait()
    own = planes[0].reshape(VOX, CHANS)
    fill_views(own, moved)
    total = jnp.zeros((VOX, CHANS), F32)
    for b in range(3):
        centre[b].wait()
        total = row_taps(total, moved, b, held.at[b])
    part_ref[...] = total
    turned_ref[0] = own.T
    loads[1].wait()
    turned_ref[1] = jnp.maximum(planes[1].reshape(VOX, CHANS), 0).T
    loads[2].wait()
    turned_ref[2] = planes[2].reshape(VOX, CHANS).T
    for copy in outer:
        copy.wait()


def early(own, pre, first, weight):
    return pl.pallas_call(
        early_kernel,
        out_shape=[
            jax.ShapeDtypeStruct((VOX, CHANS), F32),
            jax.ShapeDtypeStruct((6, CHANS, 3 * CHANS), BF16),
            jax.ShapeDtypeStruct((3, CHANS, VOX), BF16),
        ],
        in_specs=[pl.BlockSpec(memory_space=pltpu.HBM)] * 4,
        out_specs=[VMEM] * 3,
        scratch_shapes=[
            pltpu.VMEM((3, ROWS, COLS, CHANS), BF16),
            pltpu.VMEM((3, CHANS, 3 * CHANS), BF16),
            pltpu.VMEM((3, VOX + 2 * COLS, CHANS), BF16),
            pltpu.SemaphoreType.DMA((3,)),
            pltpu.SemaphoreType.DMA((3,)),
            pltpu.SemaphoreType.DMA((6,)),
        ],
        compiler_params=PARAMS,
        cost_estimate=pl.CostEstimate(
            flops=2 * VOX * 9 * CHANS * CHANS, bytes_accessed=5 * 1024 * 1024, transcendentals=0
        ),
        name="early",
    )(own, pre, first, weight)


def late_kernel(low_ref, high_ref, part_ref, kept_ref, turned_ref, out_ref, moved):
    total = part_ref[...]
    for side, source in enumerate((high_ref, low_ref)):
        fill_views(source[...].reshape(VOX, CHANS), moved.at[side])
        for b in range(3):
            total = row_taps(total, moved.at[side], b, kept_ref.at[side * 3 + b])
    second = turned_ref[1]
    hidden = jnp.where(second > 0, total.T, 0.0).astype(BF16)
    grad, first = turned_ref[0], turned_ref[2]
    for x in range(4):
        for yh in range(2):
            dest = (x * 2 + yh) * 2
            for c, (left, right) in enumerate(((grad, second), (hidden, first))):
                out_ref[dest + c, 0:OUTS] = left[OUTS * x : OUTS * (x + 1)]
                out_ref[dest + c, OUTS : OUTS + INS] = right[INS * yh : INS * (yh + 1)]


def late(low, high, part, kept, turned):
    return pl.pallas_call(
        late_kernel,
        out_shape=jax.ShapeDtypeStruct((PLANES, OUTS + INS, VOX), BF16),
        in_specs=[VMEM] * 5,
        out_specs=VMEM,
        scratch_shapes=[pltpu.VMEM((2, 3, VOX + 2 * COLS, CHANS), BF16)],
        compiler_params=PARAMS,
        cost_estimate=pl.CostEstimate(
            flops=2 * VOX * 18 * CHANS * CHANS, bytes_accessed=3 * 1024 * 1024, transcendentals=0
        ),
        name="late",
    )(low, high, part, kept, turned)


def weight_grad_kernel(given_ref, out_ref, grads, acts):
    col = lax.broadcasted_iota(jnp.int32, (INS, VOX), 1) % COLS
    row = lax.broadcasted_iota(jnp.int32, (OUTS, VOX), 1) // COLS
    for plane in range(PLANES):
        here = slice(plane * VOX, (plane + 1) * VOX)
        act = given_ref[plane, OUTS : OUTS + INS]
        wide = act.astype(F32)
        acts[0:INS, here] = jnp.where(col > 0, shifted(wide, -1, 1), 0.0).astype(BF16)
        acts[INS : 2 * INS, here] = act
        acts[2 * INS : 3 * INS, here] = jnp.where(
            col < COLS - 1, shifted(wide, 1, 1), 0.0
        ).astype(BF16)
        grad = given_ref[plane, 0:OUTS]
        wide = grad.astype(F32)
        views = (
            jnp.where(row < ROWS - 1, shifted(wide, COLS, 1), 0.0).astype(BF16),
            grad,
            jnp.where(row > 0, shifted(wide, -COLS, 1), 0.0).astype(BF16),
        )
        for a in range(3):
            there = plane + a - 1
            if 0 <= there < PLANES:
                for b in range(3):
                    top = (a * 3 + b) * OUTS
                    grads[top : top + OUTS, there * VOX : (there + 1) * VOX] = views[b]
    blank = jnp.zeros((3 * OUTS, VOX), BF16)
    grads[0 : 3 * OUTS, (PLANES - 1) * VOX : PLANES * VOX] = blank
    grads[6 * OUTS : 9 * OUTS, 0:VOX] = blank
    total = lax.dot_general(
        grads[...], acts[...], (((1,), (1,)), ((), ())), preferred_element_type=F32
    )
    peak = jnp.max(jnp.abs(total), axis=0, keepdims=True)
    peak = jnp.max(peak, axis=1, keepdims=True)
    power = jnp.ceil(jnp.log2(jnp.maximum(peak, 2.0**-100)))
    total = total * jnp.exp2(TOP - power)
    tag = jnp.broadcast_to(power, (PIECE - DATA, 128))
    for part in range(4):
        lines = jnp.concatenate(
            [
                total[k * OUTS + part * 16 : k * OUTS + part * 16 + 16, c * INS : (c + 1) * INS]
                for k in range(9)
                for c in range(3)
            ],
            axis=0,
        )
        for zl in range(4):
            for yl in range(2):
                start = (zl * 2 + yl) * DATA
                dest = ((zl * 2 + part // 2) * 2 + yl) * 2 + part % 2
                out_ref[dest] = jnp.concatenate([lines[start : start + DATA], tag], axis=0)


def weight_grad(given):
    return pl.pallas_call(
        weight_grad_kernel,
        out_shape=jax.ShapeDtypeStruct((32, PIECE, 128), F32),
        in_specs=[VMEM],
        out_specs=VMEM,
        scratch_shapes=[
            pltpu.VMEM((9 * OUTS, PLANES * VOX), BF16),
            pltpu.VMEM((3 * INS, PLANES * VOX), BF16),
        ],
        compiler_params=PARAMS,
        cost_estimate=pl.CostEstimate(
            flops=2 * 27 * OUTS * INS * PLANES * VOX, bytes_accessed=4 * 1024 * 1024, transcendentals=0
        ),
        name="weight_grad",
    )(given)


def merge_kernel(parts_ref, out_ref):
    tags = [parts_ref[source, DATA : DATA + 1, 0:1] for source in range(32)]
    peak = tags[0]
    for tag in tags[1:]:
        peak = jnp.maximum(peak, tag)
    peak = peak + 3.0
    line = lax.broadcasted_iota(jnp.int32, (PIECE, 128), 0)
    for q in range(4):
        sources = [zl * 8 + (q // 2) * 4 + yl * 2 + q % 2 for zl in range(4) for yl in range(2)]
        total = jnp.zeros((PIECE, 128), F32)
        for source in sources:
            total = total + parts_ref[source] * jnp.exp2(tags[source] - peak)
        out_ref[q * PIECE : (q + 1) * PIECE] = jnp.where(line < DATA, total, peak)


def merge(parts):
    return pl.pallas_call(
        merge_kernel,
        out_shape=jax.ShapeDtypeStruct((4 * PIECE, 128), F32),
        in_specs=[VMEM],
        out_specs=VMEM,
        compiler_params=PARAMS,
        name="merge",
    )(parts)


def finish_kernel(sums_ref, out_ref):
    scales = [jnp.exp2(sums_ref[z, DATA : DATA + 1, 0:1] - TOP) for z in range(8)]
    for q in range(4):
        total = jnp.zeros((PIECE, 128), F32)
        for z in range(8):
            total = total + sums_ref[z, q * PIECE : (q + 1) * PIECE] * scales[z]
        total = total.astype(BF16)
        for dest in range(8):
            out_ref[dest, q] = total


def finish(sums):
    return pl.pallas_call(
        finish_kernel,
        out_shape=jax.ShapeDtypeStruct((8, 4, PIECE, 128), BF16),
        in_specs=[VMEM],
        out_specs=VMEM,
        compiler_params=PARAMS,
        name="finish",
    )(sums)


def unpack_kernel(pieces_ref, *out_refs):
    for c, out_ref in enumerate(out_refs):
        for yh in range(2):
            lines = jnp.concatenate(
                [pieces_ref[piece, yh * 2 + c].astype(F32)[0:DATA] for piece in range(8)], axis=0
            )
            for tap in range(27):
                start = tap * CHANS + yh * INS
                out_ref[:, start : start + INS] = lines[tap * 16 : (tap + 1) * 16]


def unpack(pieces):
    return pl.pallas_call(
        unpack_kernel,
        out_shape=[jax.ShapeDtypeStruct((16, 27 * CHANS), F32)] * 2,
        in_specs=[VMEM],
        out_specs=[VMEM] * 2,
        compiler_params=PARAMS,
        name="unpack",
    )(pieces)


def local(layer_input, hidden_pre, out_grad, weight_second):
    mp = ("x", "yh", "c")
    own = out_grad.reshape(ROWS, COLS, CHANS)
    pre = hidden_pre.reshape(ROWS, COLS, CHANS)
    first = layer_input.reshape(ROWS, COLS, CHANS)
    up = [(i, i + 1) for i in range(PLANES - 1)]
    low = lax.ppermute(own, mp, up)
    high = lax.ppermute(own, mp, [(b, a) for a, b in up])
    kept = [pltpu.with_memory_space_constraint(a, pltpu.HBM) for a in (own, pre, first)]
    given = late(low, high, *early(*kept, weight_second))
    given = lax.all_to_all(given, mp, 0, 0, tiled=True)
    parts = weight_grad(given).astype(F16)
    parts = lax.all_to_all(parts, ("zl", "yh", "yl", "c"), 0, 0, tiled=True)
    mine = merge(parts.astype(F32)).astype(F16)
    sums = lax.all_gather(mine, "zh", axis=0, tiled=True).reshape(8, 4 * PIECE, 128)
    pieces = lax.all_to_all(finish(sums.astype(F32)), ("zl", "yl"), 0, 0, tiled=True)
    return tuple(unpack(pieces))


def solution(mesh):
    split = Mesh(mesh.devices.reshape(8, 4, 2, 4, 2, 2), ("zh", "zl", "yl", "x", "yh", "c"))
    dp, mp = ("zh", "zl", "yl"), ("x", "yh", "c")
    return jax.shard_map(
        local,
        mesh=split,
        in_specs=(P(dp, mp), P(dp, mp), P(dp, mp), P()),
        out_specs=(P(mp, None), P(mp, None)),
        check_vma=False,
    )
```

time: 146 us -> 135 us (0.925)
  blocking collectives: 119 us -> 113 us
  local copies, waits for them, and re-layouts: 2.71 us -> 0 us
  waiting for transfers between devices: 6.97 us -> 4.35 us
    all_to_all x1, blocking collectives: 37.8 us -> 32.1 us  [local(): given = lax.all_to_all(given, mp, 0, 0, tiled=True)]
    unnamed x6 -> x0, local copies, waits for them, and re-layouts: 2.71 us -> none
    ppermute x1, waiting for transfers between devices: 6.08 us -> 4.35 us  [local(): low = lax.ppermute(own, mp, up)]
    pallas_call x2 -> x3, Pallas kernels: 7.08 us -> 6.36 us  [the longest x1 2.89 us: weight_grad(): pl.pallas_call(weight_grad_kernel, out_shape=jax.ShapeDtypeStruct((32, PI...]
  transfers between devices with their start and end apart: 2 -> 2, of which waited for: 2 -> 1; matrix products, arithmetic and copies ran while one was open for 0% -> 0% of each run, Pallas kernels for 0% -> 2%
where the time goes in v3:
time: 135 us; the launch traced here: 133 us
  blocking collectives  113 us (84%)
  Pallas kernels  7.58 us (6%)
  starting transfers between devices  6.73 us (5%)
  waiting for transfers between devices  4.35 us (3%)
    all_gather x1, blocking collectives, local(): lax.all_gather(mine, 'zh', axis=0, tiled=True).reshape(8, 4 * PIECE, 128)  50.9 us
    all_to_all x1, blocking collectives, local(): given = lax.all_to_all(given, mp, 0, 0, tiled=True)  32.1 us
    all_to_all x1, blocking collectives, local(): parts = lax.all_to_all(parts, ('zl', 'yh', 'yl', 'c'), 0, 0, tiled=True)  17.7 us
    all_to_all x1, blocking collectives, local(): lax.all_to_all(finish(sums.astype(F32)), ('zl', 'yl'), 0, 0, tiled=True)  12.3 us
    ppermute x1, starting transfers between devices, local(): high = lax.ppermute(own, mp, [(b, a) for a, b in up])  4.81 us
    ppermute x1, waiting for transfers between devices, local(): low = lax.ppermute(own, mp, up)  4.35 us
    pallas_call x1, Pallas kernels, weight_grad(): pl.pallas_call(weight_grad_kernel, out_shape=jax.ShapeDtypeStruct((32, PI...  2.89 us
  transfers between devices with their start and end apart: 2, of which 1 were waited for; matrix products, arithmetic and copies ran while one was open for 0% of the time, Pallas kernels for 2%

profile of v3, /device:TPU:6, one launch (start us, length us, event | category | flops | bytes accessed | tf_op | source)
XLA Modules:
  0.0 132.6 jit_solution(17845166189457027830)
XLA Ops:
  0.6 4.8 %collective-permute-start.1 = (bf16[8,32,256]{2,1,0:T(8,128)(2,1)}, bf16[8,32,256]{2,1,0:T(8,128)(2,1)S(1)}, u32[]{:S(2)}, u32[]{:S(2)}) collective-permute-start(bf16[8,32,256]{2,1,0:T(8,128)(2,1)} %bitcast.8), channel_id=1, source_target_pairs={{1,0},{2,1},{3,2},{4,3},{5,4},{6,5},{7,6},{8,7},{9,8},{10,9},{11,1... | collective-permute-start | bytes 393224 | tf_op jit(solution)/shard_map/ppermute | solution.py:298
  5.4 1.9 %collective-permute-start = (bf16[8,32,256]{2,1,0:T(8,128)(2,1)}, bf16[8,32,256]{2,1,0:T(8,128)(2,1)S(1)}, u32[]{:S(2)}, u32[]{:S(2)}) collective-permute-start(bf16[8,32,256]{2,1,0:T(8,128)(2,1)} %bitcast.9), channel_id=1, source_target_pairs={{0,1},{1,2},{2,3},{3,4},{4,5},{5,6},{6,7},{7,8},{8,9},{9,10},{10,1... | collective-permute-start | bytes 393224 | tf_op jit(solution)/shard_map/ppermute | solution.py:297
  7.4 2.6 %early.1 = (f32[256,256]{1,0:T(8,128)S(1)}, bf16[6,256,768]{2,1,0:T(8,128)(2,1)S(1)}, bf16[3,256,256]{2,1,0:T(8,128)(2,1)S(1)}) custom-call(bf16[8,32,256]{2,1,0:T(8,128)(2,1)} %bitcast.10, bf16[8,32,256]{2,1,0:T(8,128)(2,1)} %bitcast.6, bf16[8,32,256]{2,1,0:T(8,128)(2,1)} %bitcast.7, bf16[256,6912]{1,0:T(8,128)(2,1)} %weight_ref.1), custom_call_target="tpu_custom_call" | custom-call | flops 301989888 | bytes 5242880 | tf_op jit(solution)/shard_map/early/pallas_call | solution.py:94
  10.0 0.0 collective-permute-done.1.high_ref
  10.0 4.3 %collective-permute-done.low_ref = bf16[8,32,256]{2,1,0:T(8,128)(2,1)S(1)} collective-permute-done((bf16[8,32,256]{2,1,0:T(8,128)(2,1)}, bf16[8,32,256]{2,1,0:T(8,128)(2,1)S(1)}, u32[]{:S(2)}, u32[]{:S(2)}) %collective-permute-start) | collective-permute-done | bytes 131104 | tf_op jit(solution)/shard_map/ppermute | solution.py:297
  14.3 0.9 late.1
  15.2 32.1 %all_to_all.15.given_ref = bf16[16,192,256]{2,1,0:T(8,128)(2,1)S(1)} all-to-all(bf16[16,192,256]{2,1,0:T(8,128)(2,1)S(1)} %late.1), channel_id=1, replica_groups=mesh['zh'=8,'zl'=4,'yl'=2,'x'=4,'yh'=2,'c'=2] {'x','yh','c'}, dimensions={0} | all-to-all | bytes 3145728 | tf_op jit(solution)/shard_map/all_to_all | solution.py:301
  47.4 2.9 %weight_grad.1 = f32[32,56,128]{2,1,0:T(8,128)S(1)} custom-call(bf16[16,192,256]{2,1,0:T(8,128)(2,1)S(1)} %all_to_all.15.given_ref), custom_call_target="tpu_custom_call" | custom-call | flops 1811939328 | bytes 4194304 | tf_op jit(solution)/shard_map/weight_grad/pallas_call | solution.py:204
  50.3 0.1 convert_element_type.14
  50.3 17.7 %all_to_all.16 = f16[32,56,128]{2,1,0:T(8,128)(2,1)S(1)} all-to-all(f16[32,56,128]{2,1,0:T(8,128)(2,1)S(1)} %convert_element_type.14), channel_id=1, replica_groups=mesh['zh'=8,'zl'=4,'yl'=2,'x'=4,'yh'=2,'c'=2] {'zl','yh','yl','c'}, dimensions={0} | all-to-all | bytes 917504 | tf_op jit(solution)/shard_map/all_to_all | solution.py:303
  68.0 0.1 convert_element_type.15.parts_ref
  68.1 0.1 merge.1
  68.2 50.9 %all_gather.3 = f16[1792,128]{1,0:T(8,128)(2,1)S(1)} all-gather(f16[224,128]{1,0:T(8,128)(2,1)S(1)} %convert_element_type.16), channel_id=1, replica_groups=mesh['zh'=8,'zl'=4,'yl'=2,'x'=4,'yh'=2,'c'=2] {'zh'}, dimensions={0}, use_global_device_ids=true | all-gather | bytes 516096 | tf_op jit(solution)/shard_map/all_gather | solution.py:305
  119.2 0.1 convert.1.sums_ref
  119.2 0.1 finish.1
  119.4 12.3 %all_to_all.17.pieces_ref = bf16[8,4,56,128]{3,2,1,0:T(8,128)(2,1)S(1)} all-to-all(bf16[8,4,56,128]{3,2,1,0:T(8,128)(2,1)S(1)} %finish.1), channel_id=1, replica_groups=mesh['zh'=8,'zl'=4,'yl'=2,'x'=4,'yh'=2,'c'=2] {'zl','yl'}, dimensions={0} | all-to-all | bytes 917504 | tf_op jit(solution)/shard_map/all_to_all | solution.py:306
  131.7 0.9 unpack.1
  (1 shorter events, 0.0 us)
Async XLA Ops:
  0.6 9.4 %collective-permute-start.1 = (bf16[8,32,256]{2,1,0:T(8,128)(2,1)}, bf16[8,32,256]{2,1,0:T(8,128)(2,1)S(1)}, u32[]{:S(2)}, u32[]{:S(2)}) collective-permute-start(bf16[8,32,256]{2,1,0:T(8,128)(2,1)} %bitcast.8), channel_id=1, source_target_pairs={{1,0},{2,1},{3,2},{4,3},{5,4},{6,5},{7,6},{8,7},{9,8},{10,9},{11,1... | collective-permute-start | bytes 393224 | tf_op jit(solution)/shard_map/ppermute | solution.py:298
  5.4 8.9 %collective-permute-start = (bf16[8,32,256]{2,1,0:T(8,128)(2,1)}, bf16[8,32,256]{2,1,0:T(8,128)(2,1)S(1)}, u32[]{:S(2)}, u32[]{:S(2)}) collective-permute-start(bf16[8,32,256]{2,1,0:T(8,128)(2,1)} %bitcast.9), channel_id=1, source_target_pairs={{0,1},{1,2},{2,3},{3,4},{4,5},{5,6},{6,7},{7,8},{8,9},{9,10},{10,1... | collective-permute-start | bytes 393224 | tf_op jit(solution)/shard_map/ppermute | solution.py:297

commit v4 on v3

--- a/solution.py
+++ b/solution.py
@@ -116,12 +116,13 @@
     )(own, pre, first, weight)
 
 
-def late_kernel(low_ref, high_ref, part_ref, kept_ref, turned_ref, out_ref, moved):
+def late_kernel(core_ref, near_ref, far_ref, part_ref, kept_ref, turned_ref, out_ref, moved):
+    core = core_ref[0]
     total = part_ref[...]
-    for side, source in enumerate((high_ref, low_ref)):
+    for side, (source, taps) in enumerate(((near_ref, core), (far_ref, 1 - core))):
         fill_views(source[...].reshape(VOX, CHANS), moved.at[side])
         for b in range(3):
-            total = row_taps(total, moved.at[side], b, kept_ref.at[side * 3 + b])
+            total = row_taps(total, moved.at[side], b, kept_ref.at[taps * 3 + b])
     second = turned_ref[1]
     hidden = jnp.where(second > 0, total.T, 0.0).astype(BF16)
     grad, first = turned_ref[0], turned_ref[2]
@@ -133,11 +134,11 @@
                 out_ref[dest + c, OUTS : OUTS + INS] = right[INS * yh : INS * (yh + 1)]
 
 
-def late(low, high, part, kept, turned):
+def late(core, near, far, part, kept, turned):
     return pl.pallas_call(
         late_kernel,
         out_shape=jax.ShapeDtypeStruct((PLANES, OUTS + INS, VOX), BF16),
-        in_specs=[VMEM] * 5,
+        in_specs=[pl.BlockSpec(memory_space=pltpu.SMEM)] + [VMEM] * 5,
         out_specs=VMEM,
         scratch_shapes=[pltpu.VMEM((2, 3, VOX + 2 * COLS, CHANS), BF16)],
         compiler_params=PARAMS,
@@ -145,7 +146,7 @@
             flops=2 * VOX * 18 * CHANS * CHANS, bytes_accessed=3 * 1024 * 1024, transcendentals=0
         ),
         name="late",
-    )(low, high, part, kept, turned)
+    )(core, near, far, part, kept, turned)
 
 
 def weight_grad_kernel(given_ref, out_ref, grads, acts):
@@ -293,11 +294,11 @@
     own = out_grad.reshape(ROWS, COLS, CHANS)
     pre = hidden_pre.reshape(ROWS, COLS, CHANS)
     first = layer_input.reshape(ROWS, COLS, CHANS)
-    up = [(i, i + 1) for i in range(PLANES - 1)]
-    low = lax.ppermute(own, mp, up)
-    high = lax.ppermute(own, mp, [(b, a) for a, b in up])
+    near = lax.ppermute(own, mp, [(i, i ^ 1) for i in range(PLANES)])
+    far = lax.ppermute(own, mp, [(i, i + (1 if i % 2 else -1)) for i in range(1, PLANES - 1)])
+    core = lax.axis_index("c").reshape(1)
     kept = [pltpu.with_memory_space_constraint(a, pltpu.HBM) for a in (own, pre, first)]
-    given = late(low, high, *early(*kept, weight_second))
+    given = late(core, near, far, *early(*kept, weight_second))
     given = lax.all_to_all(given, mp, 0, 0, tiled=True)
     parts = weight_grad(given).astype(F16)
     parts = lax.all_to_all(parts, ("zl", "yh", "yl", "c"), 0, 0, tiled=True)

time: 135 us -> 133 us (0.985)
  waiting for transfers between devices: 4.35 us -> 0.01 us
  blocking collectives: 113 us -> 116 us
    ppermute x2, waiting for transfers between devices: 4.35 us -> 0.01 us  [the longest x1 0.01 us: local(): lax.ppermute(own, mp, [(i, i + (1 if i % 2 else -1)) for i in range(1, PL...]
    all_gather x1, blocking collectives: 50.9 us -> 53.3 us  [local(): lax.all_gather(mine, 'zh', axis=0, tiled=True).reshape(8, 4 * PIECE, 128)]
  transfers between devices with their start and end apart: 2 -> 2, of which waited for: 1 -> 0; matrix products, arithmetic and copies ran while one was open for 0% -> 0% of each run, Pallas kernels for 2% -> 2%
where the time goes in v4:
time: 133 us; the launch traced here: 131 us
  blocking collectives  116 us (87%)
  Pallas kernels  7.58 us (6%)
  starting transfers between devices  7.13 us (5%)
    all_gather x1, blocking collectives, local(): lax.all_gather(mine, 'zh', axis=0, tiled=True).reshape(8, 4 * PIECE, 128)  53.3 us
    all_to_all x1, blocking collectives, local(): given = lax.all_to_all(given, mp, 0, 0, tiled=True)  32.4 us
    all_to_all x1, blocking collectives, local(): parts = lax.all_to_all(parts, ('zl', 'yh', 'yl', 'c'), 0, 0, tiled=True)  17.7 us
    all_to_all x1, blocking collectives, local(): lax.all_to_all(finish(sums.astype(F32)), ('zl', 'yl'), 0, 0, tiled=True)  12.3 us
    ppermute x1, starting transfers between devices, local(): lax.ppermute(own, mp, [(i, i + (1 if i % 2 else -1)) for i in range(1, PL...  4.81 us
    pallas_call x1, Pallas kernels, weight_grad(): pl.pallas_call(weight_grad_kernel, out_shape=jax.ShapeDtypeStruct((32, PI...  2.89 us
  transfers between devices with their start and end apart: 2, of which 0 were waited for; matrix products, arithmetic and copies ran while one was open for 0% of the time, Pallas kernels for 2%

profile of v4, /device:TPU:6, one launch (start us, length us, event | category | flops | bytes accessed | tf_op | source)
XLA Modules:
  0.0 131.4 jit_solution(15749479936408112525)
XLA Ops:
  0.6 4.8 %collective-permute-start.1 = (bf16[8,32,256]{2,1,0:T(8,128)(2,1)}, bf16[8,32,256]{2,1,0:T(8,128)(2,1)S(1)}, u32[]{:S(2)}, u32[]{:S(2)}) collective-permute-start(bf16[8,32,256]{2,1,0:T(8,128)(2,1)} %bitcast.9), channel_id=1, source_target_pairs={{1,2},{2,1},{3,4},{4,3},{5,6},{6,5},{7,8},{8,7},{9,10},{10,9},{11,... | collective-permute-start | bytes 393224 | tf_op jit(solution)/shard_map/ppermute | solution.py:298
  5.4 2.3 %collective-permute-start = (bf16[8,32,256]{2,1,0:T(8,128)(2,1)}, bf16[8,32,256]{2,1,0:T(8,128)(2,1)S(1)}, u32[]{:S(2)}, u32[]{:S(2)}) collective-permute-start(bf16[8,32,256]{2,1,0:T(8,128)(2,1)} %bitcast.10), channel_id=1, source_target_pairs={{0,1},{1,0},{2,3},{3,2},{4,5},{5,4},{6,7},{7,6},{8,9},{9,8},{10,11... | collective-permute-start | bytes 393224 | tf_op jit(solution)/shard_map/ppermute | solution.py:297
  7.8 2.6 %early.1 = (f32[256,256]{1,0:T(8,128)S(1)}, bf16[6,256,768]{2,1,0:T(8,128)(2,1)S(1)}, bf16[3,256,256]{2,1,0:T(8,128)(2,1)S(1)}) custom-call(bf16[8,32,256]{2,1,0:T(8,128)(2,1)} %bitcast.11, bf16[8,32,256]{2,1,0:T(8,128)(2,1)} %bitcast.7, bf16[8,32,256]{2,1,0:T(8,128)(2,1)} %bitcast.8, bf16[256,6912]{1,0:T(8,128)(2,1)} %weight_ref.1), custom_call_target="tpu_custom_call" | custom-call | flops 301989888 | bytes 5242880 | tf_op jit(solution)/shard_map/early/pallas_call | solution.py:94
  10.4 0.0 collective-permute-done.1.far_ref
  10.4 0.0 collective-permute-done.near_ref
  10.4 0.9 late.1
  11.3 32.4 %all_to_all.15.given_ref = bf16[16,192,256]{2,1,0:T(8,128)(2,1)S(1)} all-to-all(bf16[16,192,256]{2,1,0:T(8,128)(2,1)S(1)} %late.1), channel_id=1, replica_groups=mesh['zh'=8,'zl'=4,'yl'=2,'x'=4,'yh'=2,'c'=2] {'x','yh','c'}, dimensions={0} | all-to-all | bytes 3145728 | tf_op jit(solution)/shard_map/all_to_all | solution.py:302
  43.7 2.9 %weight_grad.1 = f32[32,56,128]{2,1,0:T(8,128)S(1)} custom-call(bf16[16,192,256]{2,1,0:T(8,128)(2,1)S(1)} %all_to_all.15.given_ref), custom_call_target="tpu_custom_call" | custom-call | flops 1811939328 | bytes 4194304 | tf_op jit(solution)/shard_map/weight_grad/pallas_call | solution.py:205
  46.6 0.1 convert_element_type.14
  46.7 17.7 %all_to_all.16 = f16[32,56,128]{2,1,0:T(8,128)(2,1)S(1)} all-to-all(f16[32,56,128]{2,1,0:T(8,128)(2,1)S(1)} %convert_element_type.14), channel_id=1, replica_groups=mesh['zh'=8,'zl'=4,'yl'=2,'x'=4,'yh'=2,'c'=2] {'zl','yh','yl','c'}, dimensions={0} | all-to-all | bytes 917504 | tf_op jit(solution)/shard_map/all_to_all | solution.py:304
  64.4 0.1 convert_element_type.15.parts_ref
  64.4 0.1 merge.1
  64.6 53.3 %all_gather.3 = f16[1792,128]{1,0:T(8,128)(2,1)S(1)} all-gather(f16[224,128]{1,0:T(8,128)(2,1)S(1)} %convert_element_type.16), channel_id=1, replica_groups=mesh['zh'=8,'zl'=4,'yl'=2,'x'=4,'yh'=2,'c'=2] {'zh'}, dimensions={0}, use_global_device_ids=true | all-gather | bytes 516096 | tf_op jit(solution)/shard_map/all_gather | solution.py:306
  117.9 0.1 convert.1.sums_ref
  118.0 0.1 finish.1
  118.1 12.3 %all_to_all.17.pieces_ref = bf16[8,4,56,128]{3,2,1,0:T(8,128)(2,1)S(1)} all-to-all(bf16[8,4,56,128]{3,2,1,0:T(8,128)(2,1)S(1)} %finish.1), channel_id=1, replica_groups=mesh['zh'=8,'zl'=4,'yl'=2,'x'=4,'yh'=2,'c'=2] {'zl','yl'}, dimensions={0} | all-to-all | bytes 917504 | tf_op jit(solution)/shard_map/all_to_all | solution.py:307
  130.4 0.9 unpack.1
  (1 shorter events, 0.0 us)
Async XLA Ops:
  0.6 9.8 %collective-permute-start.1 = (bf16[8,32,256]{2,1,0:T(8,128)(2,1)}, bf16[8,32,256]{2,1,0:T(8,128)(2,1)S(1)}, u32[]{:S(2)}, u32[]{:S(2)}) collective-permute-start(bf16[8,32,256]{2,1,0:T(8,128)(2,1)} %bitcast.9), channel_id=1, source_target_pairs={{1,2},{2,1},{3,4},{4,3},{5,6},{6,5},{7,8},{8,7},{9,10},{10,9},{11,... | collective-permute-start | bytes 393224 | tf_op jit(solution)/shard_map/ppermute | solution.py:298
  5.4 5.0 %collective-permute-start = (bf16[8,32,256]{2,1,0:T(8,128)(2,1)}, bf16[8,32,256]{2,1,0:T(8,128)(2,1)S(1)}, u32[]{:S(2)}, u32[]{:S(2)}) collective-permute-start(bf16[8,32,256]{2,1,0:T(8,128)(2,1)} %bitcast.10), channel_id=1, source_target_pairs={{0,1},{1,0},{2,3},{3,2},{4,5},{5,4},{6,7},{7,6},{8,9},{9,8},{10,11... | collective-permute-start | bytes 393224 | tf_op jit(solution)/shard_map/ppermute | solution.py:297

commit v5 on v4

--- a/solution.py
+++ b/solution.py
@@ -9,6 +9,7 @@
 BF16 = jnp.bfloat16
 F16 = jnp.float16
 PLANES = 16
+HALF = PLANES // 2
 ROWS = 8
 COLS = 32
 VOX = ROWS * COLS
@@ -149,11 +150,17 @@
     )(core, near, far, part, kept, turned)
 
 
-def weight_grad_kernel(given_ref, out_ref, grads, acts):
+def weight_grad_kernel(given_ref, out_ref, grads_low, grads_high, acts_low, acts_high):
+    all_grads, all_acts = (grads_low, grads_high), (acts_low, acts_high)
+    blank = jnp.zeros((3 * OUTS, VOX), BF16)
+    grads_high[0 : 3 * OUTS, (HALF - 1) * VOX : HALF * VOX] = blank
+    grads_low[6 * OUTS : 9 * OUTS, 0:VOX] = blank
+    total = None
     col = lax.broadcasted_iota(jnp.int32, (INS, VOX), 1) % COLS
     row = lax.broadcasted_iota(jnp.int32, (OUTS, VOX), 1) // COLS
     for plane in range(PLANES):
-        here = slice(plane * VOX, (plane + 1) * VOX)
+        here = slice(plane % HALF * VOX, (plane % HALF + 1) * VOX)
+        acts = all_acts[plane // HALF]
         act = given_ref[plane, OUTS : OUTS + INS]
         wide = act.astype(F32)
         acts[0:INS, here] = jnp.where(col > 0, shifted(wide, -1, 1), 0.0).astype(BF16)
@@ -171,15 +178,19 @@
         for a in range(3):
             there = plane + a - 1
             if 0 <= there < PLANES:
+                start = there % HALF * VOX
                 for b in range(3):
                     top = (a * 3 + b) * OUTS
-                    grads[top : top + OUTS, there * VOX : (there + 1) * VOX] = views[b]
-    blank = jnp.zeros((3 * OUTS, VOX), BF16)
-    grads[0 : 3 * OUTS, (PLANES - 1) * VOX : PLANES * VOX] = blank
-    grads[6 * OUTS : 9 * OUTS, 0:VOX] = blank
-    total = lax.dot_general(
-        grads[...], acts[...], (((1,), (1,)), ((), ())), preferred_element_type=F32
-    )
+                    all_grads[there // HALF][top : top + OUTS, start : start + VOX] = views[b]
+        if plane in (HALF, PLANES - 1):
+            half = 0 if plane == HALF else 1
+            term = lax.dot_general(
+                all_grads[half][...],
+                all_acts[half][...],
+                (((1,), (1,)), ((), ())),
+                preferred_element_type=F32,
+            )
+            total = term if total is None else total + term
     peak = jnp.max(jnp.abs(total), axis=0, keepdims=True)
     peak = jnp.max(peak, axis=1, keepdims=True)
     power = jnp.ceil(jnp.log2(jnp.maximum(peak, 2.0**-100)))
@@ -208,8 +219,10 @@
         in_specs=[VMEM],
         out_specs=VMEM,
         scratch_shapes=[
-            pltpu.VMEM((9 * OUTS, PLANES * VOX), BF16),
-            pltpu.VMEM((3 * INS, PLANES * VOX), BF16),
+            pltpu.VMEM((9 * OUTS, HALF * VOX), BF16),
+            pltpu.VMEM((9 * OUTS, HALF * VOX), BF16),
+            pltpu.VMEM((3 * INS, HALF * VOX), BF16),
+            pltpu.VMEM((3 * INS, HALF * VOX), BF16),
         ],
         compiler_params=PARAMS,
         cost_estimate=pl.CostEstimate(

time: 133 us -> 133 us (level)
  no operation moved by 1% of the time
where the time goes in v5:
time: 133 us; the launch traced here: 131 us
  blocking collectives  116 us (87%)
  Pallas kernels  7.58 us (6%)
  starting transfers between devices  7.13 us (5%)
    all_gather x1, blocking collectives, local(): lax.all_gather(mine, 'zh', axis=0, tiled=True).reshape(8, 4 * PIECE, 128)  53.3 us
    all_to_all x1, blocking collectives, local(): given = lax.all_to_all(given, mp, 0, 0, tiled=True)  32.4 us
    all_to_all x1, blocking collectives, local(): parts = lax.all_to_all(parts, ('zl', 'yh', 'yl', 'c'), 0, 0, tiled=True)  17.7 us
    all_to_all x1, blocking collectives, local(): lax.all_to_all(finish(sums.astype(F32)), ('zl', 'yl'), 0, 0, tiled=True)  12.3 us
    ppermute x1, starting transfers between devices, local(): lax.ppermute(own, mp, [(i, i + (1 if i % 2 else -1)) for i in range(1, PL...  4.81 us
    pallas_call x1, Pallas kernels, weight_grad(): pl.pallas_call(weight_grad_kernel, out_shape=jax.ShapeDtypeStruct((32, PI...  2.88 us
  transfers between devices with their start and end apart: 2, of which 0 were waited for; matrix products, arithmetic and copies ran while one was open for 0% of the time, Pallas kernels for 2%

profile of v5, /device:TPU:6, one launch (start us, length us, event | category | flops | bytes accessed | tf_op | source)
XLA Modules:
  0.0 131.4 jit_solution(10587401719111093841)
XLA Ops:
  0.6 4.8 %collective-permute-start.1 = (bf16[8,32,256]{2,1,0:T(8,128)(2,1)}, bf16[8,32,256]{2,1,0:T(8,128)(2,1)S(1)}, u32[]{:S(2)}, u32[]{:S(2)}) collective-permute-start(bf16[8,32,256]{2,1,0:T(8,128)(2,1)} %bitcast.9), channel_id=1, source_target_pairs={{1,2},{2,1},{3,4},{4,3},{5,6},{6,5},{7,8},{8,7},{9,10},{10,9},{11,... | collective-permute-start | bytes 393224 | tf_op jit(solution)/shard_map/ppermute | solution.py:311
  5.4 2.3 %collective-permute-start = (bf16[8,32,256]{2,1,0:T(8,128)(2,1)}, bf16[8,32,256]{2,1,0:T(8,128)(2,1)S(1)}, u32[]{:S(2)}, u32[]{:S(2)}) collective-permute-start(bf16[8,32,256]{2,1,0:T(8,128)(2,1)} %bitcast.10), channel_id=1, source_target_pairs={{0,1},{1,0},{2,3},{3,2},{4,5},{5,4},{6,7},{7,6},{8,9},{9,8},{10,11... | collective-permute-start | bytes 393224 | tf_op jit(solution)/shard_map/ppermute | solution.py:310
  7.8 2.6 %early.1 = (f32[256,256]{1,0:T(8,128)S(1)}, bf16[6,256,768]{2,1,0:T(8,128)(2,1)S(1)}, bf16[3,256,256]{2,1,0:T(8,128)(2,1)S(1)}) custom-call(bf16[8,32,256]{2,1,0:T(8,128)(2,1)} %bitcast.11, bf16[8,32,256]{2,1,0:T(8,128)(2,1)} %bitcast.7, bf16[8,32,256]{2,1,0:T(8,128)(2,1)} %bitcast.8, bf16[256,6912]{1,0:T(8,128)(2,1)} %weight_ref.1), custom_call_target="tpu_custom_call" | custom-call | flops 301989888 | bytes 5242880 | tf_op jit(solution)/shard_map/early/pallas_call | solution.py:95
  10.4 0.0 collective-permute-done.1.far_ref
  10.4 0.0 collective-permute-done.near_ref
  10.4 0.9 late.1
  11.3 32.4 %all_to_all.15.given_ref = bf16[16,192,256]{2,1,0:T(8,128)(2,1)S(1)} all-to-all(bf16[16,192,256]{2,1,0:T(8,128)(2,1)S(1)} %late.1), channel_id=1, replica_groups=mesh['zh'=8,'zl'=4,'yl'=2,'x'=4,'yh'=2,'c'=2] {'x','yh','c'}, dimensions={0} | all-to-all | bytes 3145728 | tf_op jit(solution)/shard_map/all_to_all | solution.py:315
  43.7 2.9 %weight_grad.1 = f32[32,56,128]{2,1,0:T(8,128)S(1)} custom-call(bf16[16,192,256]{2,1,0:T(8,128)(2,1)S(1)} %all_to_all.15.given_ref), custom_call_target="tpu_custom_call" | custom-call | flops 1811939328 | bytes 4194304 | tf_op jit(solution)/shard_map/weight_grad/pallas_call | solution.py:216
  46.6 0.1 convert_element_type.14
  46.7 17.7 %all_to_all.16 = f16[32,56,128]{2,1,0:T(8,128)(2,1)S(1)} all-to-all(f16[32,56,128]{2,1,0:T(8,128)(2,1)S(1)} %convert_element_type.14), channel_id=1, replica_groups=mesh['zh'=8,'zl'=4,'yl'=2,'x'=4,'yh'=2,'c'=2] {'zl','yh','yl','c'}, dimensions={0} | all-to-all | bytes 917504 | tf_op jit(solution)/shard_map/all_to_all | solution.py:317
  64.3 0.1 convert_element_type.15.parts_ref
  64.4 0.1 merge.1
  64.6 53.3 %all_gather.3 = f16[1792,128]{1,0:T(8,128)(2,1)S(1)} all-gather(f16[224,128]{1,0:T(8,128)(2,1)S(1)} %convert_element_type.16), channel_id=1, replica_groups=mesh['zh'=8,'zl'=4,'yl'=2,'x'=4,'yh'=2,'c'=2] {'zh'}, dimensions={0}, use_global_device_ids=true | all-gather | bytes 516096 | tf_op jit(solution)/shard_map/all_gather | solution.py:319
  117.9 0.1 convert.1.sums_ref
  118.0 0.1 finish.1
  118.1 12.3 %all_to_all.17.pieces_ref = bf16[8,4,56,128]{3,2,1,0:T(8,128)(2,1)S(1)} all-to-all(bf16[8,4,56,128]{3,2,1,0:T(8,128)(2,1)S(1)} %finish.1), channel_id=1, replica_groups=mesh['zh'=8,'zl'=4,'yl'=2,'x'=4,'yh'=2,'c'=2] {'zl','yl'}, dimensions={0} | all-to-all | bytes 917504 | tf_op jit(solution)/shard_map/all_to_all | solution.py:320
  130.4 0.9 unpack.1
  (1 shorter events, 0.0 us)
Async XLA Ops:
  0.6 9.8 %collective-permute-start.1 = (bf16[8,32,256]{2,1,0:T(8,128)(2,1)}, bf16[8,32,256]{2,1,0:T(8,128)(2,1)S(1)}, u32[]{:S(2)}, u32[]{:S(2)}) collective-permute-start(bf16[8,32,256]{2,1,0:T(8,128)(2,1)} %bitcast.9), channel_id=1, source_target_pairs={{1,2},{2,1},{3,4},{4,3},{5,6},{6,5},{7,8},{8,7},{9,10},{10,9},{11,... | collective-permute-start | bytes 393224 | tf_op jit(solution)/shard_map/ppermute | solution.py:311
  5.4 5.0 %collective-permute-start = (bf16[8,32,256]{2,1,0:T(8,128)(2,1)}, bf16[8,32,256]{2,1,0:T(8,128)(2,1)S(1)}, u32[]{:S(2)}, u32[]{:S(2)}) collective-permute-start(bf16[8,32,256]{2,1,0:T(8,128)(2,1)} %bitcast.10), channel_id=1, source_target_pairs={{0,1},{1,0},{2,3},{3,2},{4,5},{5,4},{6,7},{7,6},{8,9},{9,8},{10,11... | collective-permute-start | bytes 393224 | tf_op jit(solution)/shard_map/ppermute | solution.py:310
